TPU v7x, 128 devices: a whole 4x4x4 slice. The times are simulated.
128 devices in a mesh: theta: 16 (over x, y_hi, core), phi: 8 (over z, y_lo).
Axes of the slice: x: 4, y: 4 (y_hi: 2, y_lo: 2; y = y_hi * 2 + y_lo), z: 4, core: 2. Of those that a mesh axis runs over, the one named last changes fastest.
Arguments:
- child_out: float32 [8, 192, 384, 128], P(None, 'theta', 'phi'), may hold values from -6 to 6
- child_slot: int32 [128], replicated, may hold values from 0 to 127, each once
- sources_child: int32 [128, 12], replicated, may hold values from 0 to 127
- kinds_child: int32 [128, 12], replicated, may hold values from 0 to 127
- table_child: float32 [2, 192, 384, 128], P(None, 'theta', 'phi'), may hold values from -4 to 4
- sources_parent: int32 [16, 12], replicated, may hold values from 0 to 15
- kinds_parent: int32 [16, 12], replicated, may hold values from 0 to 127
- table_parent: float32 [2, 352, 704, 128], P(None, 'theta', 'phi'), may hold values from -1.5 to 1.5
Outputs:
- child_in: float32 [8, 192, 384, 128], P(None, 'theta', 'phi')
Inputs may be any that keep to these rules, and one draw needn't show every extreme that they name: Each value occurs once; child b belongs to parent child_slot[b] % 16 as octant child_slot[b] // 16.
All inputs are finite; a program needn't handle non-finite values.
Results may differ from a plain program's by a relative error of at most 0.00012.
Values sent between devices are 32-bit elements; how exact they have to be, the bound alone decides.
A program may use at most 128 MiB of HBM per device.

v0:
```python
import math

import jax
import jax.numpy as jnp
import numpy as np
from jax import lax
from jax.sharding import PartitionSpec as P

TH1 = 192
PH1 = 384
TH2 = 352
PH2 = 704
BAND1 = 180


def with_halo(block, sides, width, periodic):
    for axis, dim in sides:
        count = lax.axis_size(axis)
        forward = [(i, i + 1) for i in range(count - 1)]
        if periodic:
            forward.append((count - 1, 0))
        backward = [(target, source) for source, target in forward]
        low = lax.ppermute(
            lax.slice_in_dim(block, block.shape[dim] - width, None, axis=dim), axis, forward
        )
        high = lax.ppermute(lax.slice_in_dim(block, 0, width, axis=dim), axis, backward)
        block = jnp.concatenate([low, block, high], axis=dim)
    return block


def stencil_entries(count_out, count_in, centered, out_rows):
    entries = []
    for row_out in out_rows:
        if centered:
            numerator = (2 * row_out + 1) * count_in - count_out
        else:
            numerator = 2 * row_out * count_in
        denominator = 2 * count_out
        base_index = numerator // denominator
        fraction = (numerator - base_index * denominator) / denominator
        for offset_a in range(-2, 4):
            weight = 1.0
            for offset_b in range(-2, 4):
                if offset_b != offset_a:
                    weight = weight * (fraction - offset_b) / (offset_a - offset_b)
            entries.append((row_out, base_index + offset_a, weight))
    return entries


def local_up(count_out, count_in, centered, rows_out, rows_in):
    matrix = np.zeros((rows_out, rows_in + 6))
    for row_out, column, weight in stencil_entries(count_out, count_in, centered, range(rows_out)):
        matrix[row_out, column + 3] += weight
    return jnp.asarray(matrix, jnp.float32)


def local_down(count_out, count_in, centered, rows_out, rows_in, margin):
    matrix = np.zeros((rows_in, rows_out + 2 * margin))
    for row_out, column, weight in stencil_entries(
        count_out, count_in, centered, range(-margin, rows_out + margin)
    ):
        if 0 <= column < rows_in:
            matrix[column, row_out + margin] += weight
    return jnp.asarray(matrix, jnp.float32)


def phase_table(count_polar, count_azimuth, polar_first, azimuth_first, rows_here, columns_here):
    polar = ((jnp.arange(rows_here, dtype=jnp.int32) + polar_first).astype(jnp.float32) + 0.5) * (
        math.pi / count_polar
    )
    azimuth = (jnp.arange(columns_here, dtype=jnp.int32) + azimuth_first).astype(jnp.float32) * (
        2.0 * math.pi / count_azimuth
    )
    octant = jnp.arange(8, dtype=jnp.int32)
    east_sign = (2 * (octant % 2) - 1).astype(jnp.float32)
    north_sign = (2 * (octant // 2 % 2) - 1).astype(jnp.float32)
    upper_sign = (2 * (octant // 4) - 1).astype(jnp.float32)
    sin_polar = jnp.sin(polar)[:, None, None]
    cos_polar = jnp.cos(polar)[:, None, None]
    cos_azimuth = jnp.cos(azimuth)[None, :, None]
    sin_azimuth = jnp.sin(azimuth)[None, :, None]
    phase_angle = (
        BAND1
        / (2.0 * math.sqrt(3.0))
        * (
            sin_polar * cos_azimuth * east_sign
            + sin_polar * sin_azimuth * north_sign
            + cos_polar * upper_sign
        )
    )
    return jnp.stack([jnp.cos(phase_angle), jnp.sin(phase_angle)])


def complex_times(pattern, factor):
    halves = pattern.reshape((2, 4) + pattern.shape[1:])
    cosine = factor[0][None]
    sine_part = factor[1][None]
    real_out = halves[0] * cosine - halves[1] * sine_part
    imag_out = halves[0] * sine_part + halves[1] * cosine
    return jnp.concatenate([real_out, imag_out], axis=0)


def aggregate(grouped, phase):
    halves = grouped.reshape((2, 4) + grouped.shape[1:])
    cosine = phase[0][None, :, :, :, None]
    sine_part = phase[1][None, :, :, :, None]
    real_out = jnp.sum(halves[0] * cosine - halves[1] * sine_part, axis=3)
    imag_out = jnp.sum(halves[0] * sine_part + halves[1] * cosine, axis=3)
    return jnp.concatenate([real_out, imag_out], axis=0)


def translate(pattern, sources, kinds, table):

    def accumulate(summed, columns):
        source_column, kind_column = columns
        gathered = jnp.take(pattern, source_column, axis=3)
        factor = jnp.take(table, kind_column, axis=3)
        return (summed + complex_times(gathered, factor), None)

    start = jnp.zeros(pattern.shape[:3] + (sources.shape[0],), jnp.float32)
    summed, unused = lax.scan(accumulate, start, (sources.T, kinds.T))
    return summed


def per_device(
    child_out,
    child_slot,
    sources_child,
    kinds_child,
    table_child,
    sources_parent,
    kinds_parent,
    table_parent,
):
    exact_mode = lax.Precision.HIGHEST
    rows_child = child_out.shape[1]
    columns_child = child_out.shape[2]
    boxes_child = child_out.shape[3]
    rows_parent = table_parent.shape[1]
    columns_parent = table_parent.shape[2]
    boxes_parent = boxes_child // 8
    polar_up = local_up(TH2, TH1, True, rows_parent, rows_child)
    azimuth_up = local_up(PH2, PH1, False, columns_parent, columns_child)
    polar_index = lax.axis_index("theta")
    azimuth_index = lax.axis_index("phi")
    margin_columns = (3 * columns_parent + columns_child - 1) // columns_child + 1
    margin_rows = (3 * rows_parent + rows_child - 1) // rows_child + 1
    azimuth_down = local_down(PH2, PH1, False, columns_parent, columns_child, margin_columns)
    polar_down = local_down(TH2, TH1, True, rows_parent, rows_child, margin_rows)
    inverse = (
        jnp.zeros((boxes_child,), jnp.int32)
        .at[child_slot]
        .set(jnp.arange(boxes_child, dtype=jnp.int32))
    )
    padded = with_halo(child_out, (("theta", 1),), 3, False)
    row_pass = jnp.einsum("pt,ctfb->cpfb", polar_up, padded, precision=exact_mode)
    padded = with_halo(row_pass, (("phi", 2),), 3, True)
    upward = jnp.einsum("qf,cpfb->cpqb", azimuth_up, padded, precision=exact_mode)
    grouped = jnp.take(upward, inverse, axis=3).reshape(
        8, rows_parent, columns_parent, 8, boxes_parent
    )
    phase_up = phase_table(
        TH2,
        PH2,
        polar_index * rows_parent,
        azimuth_index * columns_parent,
        rows_parent,
        columns_parent,
    )
    parent_out = aggregate(grouped, phase_up)
    child_local = translate(child_out, sources_child, kinds_child, table_child)
    parent_in = translate(parent_out, sources_parent, kinds_parent, table_parent)
    widened = with_halo(parent_in, (("phi", 2),), margin_columns, True)
    columns_back = jnp.einsum("fq,cpqb->cpfb", azimuth_down, widened, precision=exact_mode)
    heightened = with_halo(columns_back, (("theta", 1),), margin_rows, False)
    lowered = jnp.einsum("tp,cpfb->ctfb", polar_down, heightened, precision=exact_mode)
    expanded = jnp.take(lowered, child_slot % boxes_parent, axis=3)
    phase_down = phase_table(
        TH1, PH1, polar_index * rows_child, azimuth_index * columns_child, rows_child, columns_child
    )
    octant_onehot = (
        jnp.arange(8, dtype=jnp.int32)[:, None] == (child_slot // boxes_parent)[None, :]
    ).astype(jnp.float32)
    box_phase = jnp.einsum("atfo,ob->atfb", phase_down, octant_onehot, precision=exact_mode)
    factor = jnp.stack([box_phase[0], -box_phase[1]])
    return complex_times(expanded, factor) + child_local


def solution(mesh):
    placed = (
        P(None, "theta", "phi", None),
        P(),
        P(),
        P(),
        P(None, "theta", "phi", None),
        P(),
        P(),
        P(None, "theta", "phi", None),
    )
    return jax.shard_map(
        per_device,
        mesh=mesh,
        in_specs=placed,
        out_specs=P(None, "theta", "phi", None),
        check_vma=False,
    )
```

profile of v0, /device:TPU:3, one launch (start us, length us, event | category | flops | bytes accessed | tf_op | source)
XLA Modules:
  0.0 679.8 jit_solution(9898477831797314604)
XLA Ops:
  2.5 5.4 collective-permute-start
  9.8 4.0 copy.104
  17.7 391.3 %while.23 = (s32[]{:T(128)}, f32[8,12,48,128]{3,2,1,0:T(8,128)}, s32[12,128]{1,0:T(8,128)}, f32[8,12,48,128]{2,0,3,1:T(8,128)}, s32[12,128]{1,0:T(8,128)}, /*ind...) while((s32[]{:T(128)}, f32[8,12,48,128]{3,2,1,0:T(8,128)}, s32[12,128]{1,0:T(8,128)}, ...), condition=%wide.region_6.7_spmd.clone, body=%wide.region_5.6_spmd.clone.sunk | while | flops 4280579 | bytes 38352596 | solution.py:121
  26.2 6.8 %gather_fusion.2 = f32[128,8,12,48]{3,1,2,0:T(8,128)} fusion(f32[8,12,48,128]{2,0,3,1:T(8,128)} %get-tuple-element.352, s32[1024]{0:T(1024)S(1)} %pad_clamp_fusion.12), kind=kCustom, calls=%fused_computation.2.clone.clone.1 | custom fusion | bytes 4719104 | tf_op jit(solution)/shard_map/while/body/eval_jaxpr/jit(_take)/gather | solution.py:116
  39.4 4.3 copy.137
  46.1 3.4 maximum_add_fusion.6
  58.1 6.8 %gather_fusion.2 = f32[128,8,12,48]{3,1,2,0:T(8,128)} fusion(f32[8,12,48,128]{2,0,3,1:T(8,128)} %get-tuple-element.352, s32[1024]{0:T(1024)S(1)} %pad_clamp_fusion.12), kind=kCustom, calls=%fused_computation.2.clone.clone.1 | custom fusion | bytes 4719104 | tf_op jit(solution)/shard_map/while/body/eval_jaxpr/jit(_take)/gather | solution.py:116
  64.9 3.4 select_bitcast_fusion.12
  71.3 4.3 copy.137
  78.0 4.2 maximum_add_fusion.6
  90.7 6.8 %gather_fusion.2 = f32[128,8,12,48]{3,1,2,0:T(8,128)} fusion(f32[8,12,48,128]{2,0,3,1:T(8,128)} %get-tuple-element.352, s32[1024]{0:T(1024)S(1)} %pad_clamp_fusion.12), kind=kCustom, calls=%fused_computation.2.clone.clone.1 | custom fusion | bytes 4719104 | tf_op jit(solution)/shard_map/while/body/eval_jaxpr/jit(_take)/gather | solution.py:116
  103.9 4.3 copy.137
  110.7 4.2 maximum_add_fusion.6
  123.4 6.8 %gather_fusion.2 = f32[128,8,12,48]{3,1,2,0:T(8,128)} fusion(f32[8,12,48,128]{2,0,3,1:T(8,128)} %get-tuple-element.352, s32[1024]{0:T(1024)S(1)} %pad_clamp_fusion.12), kind=kCustom, calls=%fused_computation.2.clone.clone.1 | custom fusion | bytes 4719104 | tf_op jit(solution)/shard_map/while/body/eval_jaxpr/jit(_take)/gather | solution.py:116
  130.2 3.4 select_bitcast_fusion.12
  136.6 4.3 copy.137
  143.3 4.2 maximum_add_fusion.6
  156.0 6.8 %gather_fusion.2 = f32[128,8,12,48]{3,1,2,0:T(8,128)} fusion(f32[8,12,48,128]{2,0,3,1:T(8,128)} %get-tuple-element.352, s32[1024]{0:T(1024)S(1)} %pad_clamp_fusion.12), kind=kCustom, calls=%fused_computation.2.clone.clone.1 | custom fusion | bytes 4719104 | tf_op jit(solution)/shard_map/while/body/eval_jaxpr/jit(_take)/gather | solution.py:116
  169.2 4.3 copy.137
  175.9 4.2 maximum_add_fusion.6
  188.6 6.8 %gather_fusion.2 = f32[128,8,12,48]{3,1,2,0:T(8,128)} fusion(f32[8,12,48,128]{2,0,3,1:T(8,128)} %get-tuple-element.352, s32[1024]{0:T(1024)S(1)} %pad_clamp_fusion.12), kind=kCustom, calls=%fused_computation.2.clone.clone.1 | custom fusion | bytes 4719104 | tf_op jit(solution)/shard_map/while/body/eval_jaxpr/jit(_take)/gather | solution.py:116
  195.4 3.4 select_bitcast_fusion.12
  201.8 4.3 copy.137
  208.5 4.2 maximum_add_fusion.6
  221.3 6.8 %gather_fusion.2 = f32[128,8,12,48]{3,1,2,0:T(8,128)} fusion(f32[8,12,48,128]{2,0,3,1:T(8,128)} %get-tuple-element.352, s32[1024]{0:T(1024)S(1)} %pad_clamp_fusion.12), kind=kCustom, calls=%fused_computation.2.clone.clone.1 | custom fusion | bytes 4719104 | tf_op jit(solution)/shard_map/while/body/eval_jaxpr/jit(_take)/gather | solution.py:116
  234.4 4.3 copy.137
  241.2 4.2 maximum_add_fusion.6
  253.9 6.8 %gather_fusion.2 = f32[128,8,12,48]{3,1,2,0:T(8,128)} fusion(f32[8,12,48,128]{2,0,3,1:T(8,128)} %get-tuple-element.352, s32[1024]{0:T(1024)S(1)} %pad_clamp_fusion.12), kind=kCustom, calls=%fused_computation.2.clone.clone.1 | custom fusion | bytes 4719104 | tf_op jit(solution)/shard_map/while/body/eval_jaxpr/jit(_take)/gather | solution.py:116
  267.1 4.3 copy.137
  273.8 4.2 maximum_add_fusion.6
  286.5 6.8 %gather_fusion.2 = f32[128,8,12,48]{3,1,2,0:T(8,128)} fusion(f32[8,12,48,128]{2,0,3,1:T(8,128)} %get-tuple-element.352, s32[1024]{0:T(1024)S(1)} %pad_clamp_fusion.12), kind=kCustom, calls=%fused_computation.2.clone.clone.1 | custom fusion | bytes 4719104 | tf_op jit(solution)/shard_map/while/body/eval_jaxpr/jit(_take)/gather | solution.py:116
  299.7 4.3 copy.137
  306.4 4.2 maximum_add_fusion.6
  319.1 6.8 %gather_fusion.2 = f32[128,8,12,48]{3,1,2,0:T(8,128)} fusion(f32[8,12,48,128]{2,0,3,1:T(8,128)} %get-tuple-element.352, s32[1024]{0:T(1024)S(1)} %pad_clamp_fusion.12), kind=kCustom, calls=%fused_computation.2.clone.clone.1 | custom fusion | bytes 4719104 | tf_op jit(solution)/shard_map/while/body/eval_jaxpr/jit(_take)/gather | solution.py:116
  332.3 4.3 copy.137
  339.1 4.2 maximum_add_fusion.6
  351.8 6.8 %gather_fusion.2 = f32[128,8,12,48]{3,1,2,0:T(8,128)} fusion(f32[8,12,48,128]{2,0,3,1:T(8,128)} %get-tuple-element.352, s32[1024]{0:T(1024)S(1)} %pad_clamp_fusion.12), kind=kCustom, calls=%fused_computation.2.clone.clone.1 | custom fusion | bytes 4719104 | tf_op jit(solution)/shard_map/while/body/eval_jaxpr/jit(_take)/gather | solution.py:116
  364.9 4.3 copy.137
  371.7 4.2 maximum_add_fusion.6
  384.4 6.8 %gather_fusion.2 = f32[128,8,12,48]{3,1,2,0:T(8,128)} fusion(f32[8,12,48,128]{2,0,3,1:T(8,128)} %get-tuple-element.352, s32[1024]{0:T(1024)S(1)} %pad_clamp_fusion.12), kind=kCustom, calls=%fused_computation.2.clone.clone.1 | custom fusion | bytes 4719104 | tf_op jit(solution)/shard_map/while/body/eval_jaxpr/jit(_take)/gather | solution.py:116
  397.6 4.3 copy.137
  404.3 4.2 maximum_add_fusion.6
  415.0 5.7 fusion.21
  423.4 3.6 collective-permute-start.3
  426.9 3.6 copy.94
  432.2 5.8 collective-permute-done.3
  440.8 8.6 %fusion.12 = f32[8,22,88,128]{3,2,1,0:T(8,128)} fusion(f32[88,54,1,1]{0,1,3,2:T(8,128)S(1)} %copy-done.12, f32[8,22,54,128]{3,1,2,0:T(8,128)S(1)} %pad_maximum_fusion), kind=kOutput, calls=%fused_computation.60 | convolution fusion | flops 1284636672 | bytes 12814912 | tf_op jit(solution)/shard_map/qf,cpfb->cpqb/dot_general | solution.py:158
  449.4 11.2 %copy.89 = f32[8,22,88,128]{2,1,0,3:T(8,128)} copy(f32[8,22,88,128]{3,2,1,0:T(8,128)} %fusion.12) | data formatting | bytes 15859712 | tf_op jit(solution)/shard_map/qf,cpfb->cpqb/transpose | solution.py:158
  460.6 10.5 %gather_fusion.4 = f32[128,8,22,88]{3,2,1,0:T(8,128)} fusion(f32[8,22,88,128]{2,1,0,3:T(8,128)} %copy.89, s32[1024]{0:T(1024)S(1)} %pad_clamp_fusion.5), kind=kCustom, calls=%fused_computation.4 | custom fusion | bytes 15860224 | tf_op jit(solution)/shard_map/jit(_take)/gather | solution.py:159
  471.0 11.8 %select_bitcast_fusion.4 = f32[8,22,88,128]{2,1,0,3:T(8,128)} fusion(f32[128,8,22,88]{3,2,1,0:T(8,128)} %gather_fusion.4, pred[128]{0:T(512)(128)(4,1)S(1)} %compare_and_fusion.4), kind=kLoop, calls=%fused_computation.45 | loop fusion | flops 1982464 | bytes 15859840 | tf_op jit(solution)/shard_map/jit(_take)/select_n | solution.py:159
  482.8 8.6 %fusion.74 = (f32[4,22,88,128]{2,1,0,3:T(8,128)}, f32[4,22,88,128]{2,1,0,3:T(8,128)S(1)}) fusion(f32[8,22,88,128]{2,1,0,3:T(8,128)} %select_bitcast_fusion.4), kind=kLoop, calls=%fused_computation.153 | loop fusion | bytes 15859712 | tf_op jit(solution)/shard_map/slice | solution.py:107
  491.4 6.1 copy.90
  504.5 92.5 %while.22 = (s32[]{:T(128)}, f32[8,22,88,16]{2,0,1,3:T(8,128)}, s32[12,16]{1,0:T(8,128)S(1)}, f32[8,22,88,16]{2,0,3,1:T(8,128)S(1)}, s32[12,16]{1,0:T(8,128)S(1)...) while((s32[]{:T(128)}, f32[8,22,88,16]{2,0,1,3:T(8,128)}, s32[12,16]{1,0:T(8,128)S(1)}, ...), condition=%wide.region_4.5_spmd.clone, body=%wide.region_3.4_spmd.clone.sunk | while | flops 1798947 | bytes 11160359 | solution.py:121
  597.1 4.6 copy.95
  603.1 3.6 collective-permute-start.5
  607.7 7.5 %collective-permute-done.4 = f32[8,22,7,16]{1,3,2,0:T(8,128)} collective-permute-done((f32[8,22,7,16]{1,3,2,0:T(8,128)S(1)}, f32[8,22,7,16]{1,3,2,0:T(8,128)}, u32[]{:S(2)}, u32[]{:S(2)}) %collective-permute-start.4) | collective-permute-done | bytes 78880 | tf_op jit(solution)/shard_map/ppermute | solution.py:23
  618.3 6.0 collective-permute-done.5
  627.3 3.7 fusion.30
  631.2 4.8 collective-permute-start.6
  642.1 10.1 %collective-permute-done.7 = f32[8,7,48,16]{2,1,3,0:T(8,128)} collective-permute-done((f32[8,7,48,16]{2,1,3,0:T(8,128)S(1)}, f32[8,7,48,16]{2,1,3,0:T(8,128)}, u32[]{:S(2)}, u32[]{:S(2)}) %collective-permute-start.7) | collective-permute-done | bytes 172064 | tf_op jit(solution)/shard_map/ppermute | solution.py:26
  655.3 4.4 gather_fusion.5
  659.7 4.2 select_bitcast_fusion.5
  663.9 4.9 multiply_subtract_fusion.2
  672.1 4.3 copy.103
  (480 shorter events, 340.7 us)
Async XLA Ops:
  0.0 9.8 %copy-start.5 = (f32[8,12,48,128]{3,2,1,0:T(8,128)S(1)}, f32[8,12,48,128]{3,2,1,0:T(8,128)}, u32[]{:S(2)}) copy-start(f32[8,12,48,128]{3,2,1,0:T(8,128)} %param.16) | copy-start | bytes 7077892
  2.5 409.7 %collective-permute-start = (f32[8,3,48,128]{3,2,1,0:T(8,128)}, f32[8,3,48,128]{3,2,1,0:T(8,128)}, u32[]{:S(2)}, u32[]{:S(2)}) collective-permute-start(f32[8,3,48,128]{3,2,1,0:T(8,128)} %get-tuple-element.201), channel_id=1, source_target_pairs={{0,8},{8,16},{16,24},{24,32},{32,40},{40,48},{48,56},{56,64},{64,7... | collective-permute-start | bytes 1769480 | tf_op jit(solution)/shard_map/ppermute | solution.py:23
  7.9 405.7 %collective-permute-start.1 = (f32[8,3,48,128]{3,2,1,0:T(8,128)}, f32[8,3,48,128]{3,2,1,0:T(8,128)}, u32[]{:S(2)}, u32[]{:S(2)}) collective-permute-start(f32[8,3,48,128]{3,2,1,0:T(8,128)} %get-tuple-element.202), channel_id=1, source_target_pairs={{8,0},{16,8},{24,16},{32,24},{40,32},{48,40},{56,48},{64,56},{72,6... | collective-permute-start | bytes 1769480 | tf_op jit(solution)/shard_map/ppermute | solution.py:26
  9.8 4.1 copy-start.18
  17.7 6.4 copy-start.6
  33.1 3.4 copy-start
  33.1 3.4 copy-start.1
  46.1 3.4 copy-start.7
  49.6 6.4 copy-start.6
  64.9 3.4 copy-start
  64.9 3.4 copy-start.1
  78.0 4.2 copy-start.7
  82.2 6.4 copy-start.6
  97.6 3.4 copy-start
  97.6 3.4 copy-start.1
  110.7 4.2 copy-start.7
  114.9 6.4 copy-start.6
  130.2 3.4 copy-start
  130.2 3.4 copy-start.1
  143.3 4.2 copy-start.7
  147.5 6.4 copy-start.6
  162.8 3.4 copy-start.1
  175.9 4.2 copy-start.7
  180.1 6.4 copy-start.6
  195.4 3.4 copy-start.1
  208.5 4.2 copy-start.7
  212.7 6.4 copy-start.6
  228.1 3.4 copy-start.1
  241.2 4.2 copy-start.7
  245.4 6.4 copy-start.6
  260.7 3.4 copy-start.1
  273.8 4.2 copy-start.7
  278.0 6.4 copy-start.6
  293.3 3.4 copy-start
  293.3 3.4 copy-start.1
  306.4 4.2 copy-start.7
  310.6 6.4 copy-start.6
  326.0 3.4 copy-start.1
  339.0 4.2 copy-start.7
  343.2 6.4 copy-start.6
  358.6 3.4 copy-start.1
  371.7 4.2 copy-start.7
  375.9 6.4 copy-start.6
  391.2 3.4 copy-start.1
  404.3 4.2 copy-start.7
  409.1 5.9 copy-start.14
  415.0 11.9 %copy-start.11 = (f32[2,22,88,128]{3,2,1,0:T(8,128)S(1)}, f32[2,22,88,128]{3,2,1,0:T(8,128)}, u32[]{:S(2)}) copy-start(f32[2,22,88,128]{3,2,1,0:T(8,128)} %param.23) | copy-start | bytes 5947396
  422.9 7.7 %copy-start.16 = (s32[16,12]{1,0:T(8,128)S(1)}, s32[16,12]{1,0:T(8,128)}, u32[]{:S(2)}) copy-start(s32[16,12]{1,0:T(8,128)} %param.21) | copy-start | bytes 2308
  422.9 7.8 %copy-start.17 = (s32[16,12]{1,0:T(8,128)S(1)}, s32[16,12]{1,0:T(8,128)}, u32[]{:S(2)}) copy-start(s32[16,12]{1,0:T(8,128)} %param.22) | copy-start | bytes 2308
  422.9 9.3 %collective-permute-start.2 = (f32[8,22,3,128]{3,1,2,0:T(8,128)S(1)}, f32[8,22,3,128]{3,1,2,0:T(8,128)S(1)}, u32[]{:S(2)}, u32[]{:S(2)}) collective-permute-start(f32[8,22,3,128]{3,1,2,0:T(8,128)S(1)} %get-tuple-element.199), channel_id=1, source_target_pairs={{0,1},{1,2},{2,3},{3,4},{4,5},{5,6},{6,7},{7,0},{8,9},{9,10},{10,1... | collective-permute-start | bytes 811016 | tf_op jit(solution)/shard_map/ppermute | solution.py:23
  423.4 14.6 %collective-permute-start.3 = (f32[8,22,3,128]{3,1,2,0:T(8,128)S(1)}, f32[8,22,3,128]{3,1,2,0:T(8,128)}, u32[]{:S(2)}, u32[]{:S(2)}) collective-permute-start(f32[8,22,3,128]{3,1,2,0:T(8,128)S(1)} %get-tuple-element.200), channel_id=1, source_target_pairs={{1,0},{2,1},{3,2},{4,3},{5,4},{6,5},{7,6},{0,7},{9,8},{10,9},{11,1... | collective-permute-start | bytes 811016 | tf_op jit(solution)/shard_map/ppermute | solution.py:26
  432.2 8.6 %copy-start.12 = (f32[88,54,1,1]{0,1,3,2:T(8,128)S(1)}, f32[88,54,1,1]{0,1,3,2:T(8,128)}, u32[]{:S(2)}) copy-start(f32[88,54,1,1]{0,1,3,2:T(8,128)} %constant.237) | copy-start | bytes 57028
  597.1 9.6 %copy-start.10 = (f32[2,12,48,128]{3,2,1,0:T(8,128)S(1)}, f32[2,12,48,128]{3,2,1,0:T(8,128)}, u32[]{:S(2)}) copy-start(f32[2,12,48,128]{3,2,1,0:T(8,128)} %fusion.37) | copy-start | bytes 1769476
  601.7 5.7 copy-start.3
  603.0 12.2 %collective-permute-start.4 = (f32[8,22,7,16]{1,3,2,0:T(8,128)S(1)}, f32[8,22,7,16]{1,3,2,0:T(8,128)}, u32[]{:S(2)}, u32[]{:S(2)}) collective-permute-start(f32[8,22,7,16]{1,3,2,0:T(8,128)S(1)} %get-tuple-element.197), channel_id=1, source_target_pairs={{0,1},{1,2},{2,3},{3,4},{4,5},{5,6},{6,7},{7,0},{8,9},{9,10},{10,1... | collective-permute-start | bytes 236552 | tf_op jit(solution)/shard_map/ppermute | solution.py:23
  603.1 21.1 %collective-permute-start.5 = (f32[8,22,7,16]{1,3,2,0:T(8,128)S(1)}, f32[8,22,7,16]{1,3,2,0:T(8,128)}, u32[]{:S(2)}, u32[]{:S(2)}) collective-permute-start(f32[8,22,7,16]{1,3,2,0:T(8,128)S(1)} %get-tuple-element.198), channel_id=1, source_target_pairs={{1,0},{2,1},{3,2},{4,3},{5,4},{6,5},{7,6},{0,7},{9,8},{10,9},{11,1... | collective-permute-start | bytes 236552 | tf_op jit(solution)/shard_map/ppermute | solution.py:26
  607.4 19.9 %copy-start.13 = (f32[48,102,1,1]{1,0,3,2:T(8,128)S(1)}, f32[48,102,1,1]{1,0,3,2:T(8,128)}, u32[]{:S(2)}) copy-start(f32[48,102,1,1]{1,0,3,2:T(8,128)} %constant.238) | copy-start | bytes 58756
  627.3 11.0 %copy-start.19 = (s32[128]{0:T(128)S(1)}, s32[128]{0:T(128)}, u32[]{:S(2)}) copy-start(s32[128]{0:T(128)} %param.17) | copy-start | bytes 1540
  631.0 21.1 %copy-start.15 = (f32[12,36,1,1]{1,0,3,2:T(8,128)S(1)}, f32[12,36,1,1]{1,0,3,2:T(8,128)}, u32[]{:S(2)}) copy-start(f32[12,36,1,1]{1,0,3,2:T(8,128)} %constant.239) | copy-start | bytes 5188
  631.2 10.9 %collective-permute-start.6 = (f32[8,7,48,16]{2,1,3,0:T(8,128)S(1)}, f32[8,7,48,16]{2,1,3,0:T(8,128)S(1)}, u32[]{:S(2)}, u32[]{:S(2)}) collective-permute-start(f32[8,7,48,16]{2,1,3,0:T(8,128)S(1)} %get-tuple-element.203), channel_id=1, source_target_pairs={{0,8},{8,16},{16,24},{24,32},{32,40},{40,48},{48,56},{56,64},{64,7... | collective-permute-start | bytes 516104 | tf_op jit(solution)/shard_map/ppermute | solution.py:23
  636.0 16.2 %collective-permute-start.7 = (f32[8,7,48,16]{2,1,3,0:T(8,128)S(1)}, f32[8,7,48,16]{2,1,3,0:T(8,128)}, u32[]{:S(2)}, u32[]{:S(2)}) collective-permute-start(f32[8,7,48,16]{2,1,3,0:T(8,128)S(1)} %get-tuple-element.204), channel_id=1, source_target_pairs={{8,0},{16,8},{24,16},{32,24},{40,32},{48,40},{56,48},{64,56},{72,6... | collective-permute-start | bytes 516104 | tf_op jit(solution)/shard_map/ppermute | solution.py:26
  659.7 4.2 copy-start.8
  659.7 4.2 copy-start.9
  672.1 4.3 copy-start.2
  (8 other events, 26.2 us)
where the time goes:
time: 691 us; the launch traced here: 680 us
  local copies, waits for them, and re-layouts  375 us (54%)
  other arithmetic  228 us (33%)
  waiting for transfers between devices  29.3 us (4%)
  matrix products  22.6 us (3%)
  starting transfers between devices  22.1 us (3%)
    gather x24, local copies, waits for them, and re-layouts, accumulate(): gathered = jnp.take(pattern, source_column, axis=3)  90.5 us
    add x24, other arithmetic, accumulate(): return (summed + complex_times(gathered, factor), None)  83.8 us
    gather x24, local copies, waits for them, and re-layouts, accumulate(): factor = jnp.take(table, kind_column, axis=3)  69.5 us
    add x13, local copies, waits for them, and re-layouts, complex_times(): imag_out = halves[0] * sine_part + halves[1] * cosine  55.9 us
    select_n x48, other arithmetic, accumulate(): gathered = jnp.take(pattern, source_column, axis=3)  52.2 us
    sub x25, other arithmetic, complex_times(): real_out = halves[0] * cosine - halves[1] * sine_part  44.9 us
    sub x13, local copies, waits for them, and re-layouts, complex_times(): real_out = halves[0] * cosine - halves[1] * sine_part  32.3 us
    mul x50, local copies, waits for them, and re-layouts, complex_times(): real_out = halves[0] * cosine - halves[1] * sine_part  29.6 us
  transfers between devices with their start and end apart: 8, of which 4 were waited for; matrix products, arithmetic and copies ran while one was open for 61% of the time, Pallas kernels for 0%

commit v1 on v0

v1 whole, which is shorter than its diff:
```python
import functools
import math

import jax
import jax.numpy as jnp
import numpy as np
from jax import lax
from jax.experimental import pallas as pl
from jax.experimental.pallas import tpu as pltpu
from jax.sharding import PartitionSpec as P

TH1, PH1, TH2, PH2 = 192, 384, 352, 704
BAND1 = 180
LIST = 12
T1, F1, T2, F2 = 12, 48, 22, 88
QX = 96
NB = 128
ROWS = 32
WAVE = BAND1 / (2.0 * math.sqrt(3.0))
F32, BF16 = jnp.float32, jnp.bfloat16
MESH = pl.DeviceIdType.MESH
VM = pl.BlockSpec(memory_space=pltpu.VMEM)
SM = pl.BlockSpec(memory_space=pltpu.SMEM)


def stencil(count_out, count_in, centered, row_out):
    if centered:
        numerator = (2 * row_out + 1) * count_in - count_out
    else:
        numerator = 2 * row_out * count_in
    denominator = 2 * count_out
    base = numerator // denominator
    fraction = (numerator - base * denominator) / denominator
    weights = []
    for a in range(-2, 4):
        weight = 1.0
        for b in range(-2, 4):
            if b != a:
                weight = weight * (fraction - b) / (a - b)
        weights.append(weight)
    return base, weights


def as_halves(matrix):
    matrix = np.asarray(matrix, np.float32)
    high = matrix.astype(BF16)
    low = (matrix - high.astype(np.float32)).astype(BF16)
    return high, low


def parent_columns():
    return list(range(F2)) + [89, 90, 91, -5, -4, -3, -2, -1]


def child_columns():
    return list(range(F1)) + [48, 49, 50, None, None, -3, -2, -1]


def theta_weights():
    weight = np.zeros((ROWS * 6,), np.float32)
    for r in range(ROWS):
        base, weights = stencil(TH2, TH1, True, r - 5)
        for m in range(6):
            weight[r * 6 + m] = weights[m] if 0 <= base - 2 + m < T1 else 0.0
    return weight


def phi_up():
    matrix = np.zeros((QX, F1))
    for row, q in enumerate(parent_columns()):
        base, weights = stencil(PH2, PH1, False, q)
        for m in range(6):
            f = base - 2 + m
            if 0 <= f < F1:
                matrix[row, f] += weights[m]
    high, low = as_halves(matrix)
    return np.concatenate([high, high, low], axis=1)


def phi_down():
    matrix = np.zeros((56, 96))
    where = {f: row for row, f in enumerate(child_columns()) if f is not None}
    for q in range(F2):
        base, weights = stencil(PH2, PH1, False, q)
        for m in range(6):
            if weights[m] != 0.0:
                matrix[where[base - 2 + m], q] += weights[m]
    high, low = as_halves(matrix)
    return np.concatenate([high, high, low], axis=1)


def theta_down():
    slots = {}
    for t in range(T1):
        slots[t] = t
    for t in range(3):
        slots[12 + t] = 16 + t
        slots[t - 3] = 21 + t
    matrix = np.zeros((24, 24))
    for p in range(T2):
        base, weights = stencil(TH2, TH1, True, p)
        for m in range(6):
            matrix[p, slots[base - 2 + m]] += weights[m]
    big = np.kron(matrix, np.eye(16))
    high, low = as_halves(big)
    parts = []
    for tile in range(3):
        cut = slice(128 * tile, 128 * tile + 128)
        parts += [high[cut], high[cut], low[cut]]
    return np.concatenate(parts, axis=0)


def halves(x):
    high = x.astype(BF16)
    return high, (x - high.astype(F32)).astype(BF16)


def iota(shape, dim):
    return lax.broadcasted_iota(jnp.int32, shape, dim)


def flags(condition):
    return jnp.where(condition, 1.0, 0.0).astype(BF16)


def ring_phase(index, shift, period):
    value = index - shift
    value = jnp.where(value >= period, value - period, value)
    value = jnp.where(value >= period, value - period, value)
    value = jnp.where(value < 0, value + period, value)
    value = jnp.where(value < 0, value + period, value)
    angle = (value.astype(F32) + 0.5) * (2.0 * math.pi / period)
    phase = (WAVE / math.sqrt(2.0)) * jnp.sin(angle)
    return jnp.cos(phase), jnp.sin(phase)


def octant_shift(octant, eighth):
    east = octant % 2
    north = (octant // 2) % 2
    quarter = jnp.where(east == 1, eighth, 3 * eighth)
    return jnp.where(north == 1, quarter, -quarter)


def fill_phases(slot, tables, rows, first_plus, first_minus, polar_first, polar_rows, period):
    plus_c, plus_s, minus_c, minus_s, polar_c, polar_s = tables
    octant = jnp.broadcast_to(slot // 16, (rows, NB))
    shift = octant_shift(octant, period // 8)
    row = iota((rows, NB), 0)
    plus_c[...], plus_s[...] = ring_phase(row + first_plus, shift, period)
    minus_c[...], minus_s[...] = ring_phase(-(row + first_minus), -shift, period)
    upper = jnp.broadcast_to(slot // 64, (polar_rows, NB))
    sign = jnp.where(upper == 1, WAVE, -WAVE)
    polar = (iota((polar_rows, NB), 0) + polar_first).astype(F32) + 0.5
    phase = sign * jnp.cos(polar * (2.0 * math.pi / period))
    polar_c[...] = jnp.cos(phase)
    polar_s[...] = jnp.sin(phase)


def times(ar, ai, br, bi):
    return ar * br - ai * bi, ar * bi + ai * br


INDEX_ROWS = NB + 40


def index_kernel(slot_ref, sc_ref, kc_ref, sp_ref, kp_ref, o_ref, wide):
    o_ref[0:NB, :] = jnp.broadcast_to(slot_ref[...], (NB, NB)).T
    o_ref[NB : NB + 8, :] = jnp.broadcast_to(slot_ref[...], (8, NB))
    lane, row = iota((16, NB), 1), iota((16, NB), 0)
    wide[...] = jnp.zeros_like(wide)
    for n, ref in enumerate((sc_ref, kc_ref)):
        wide[:, 0:LIST] = ref[...]
        o_ref[NB + 8 + 16 * n : NB + 24 + 16 * n, :] = wide[...].T[0:16]
    wide[...] = jnp.zeros_like(wide)
    for n, ref in enumerate((sp_ref, kp_ref)):
        wide[0:16, 0:LIST] = ref[...]
        turned = wide[...].T[0:16].astype(F32)
        for step in (16, 32, 64):
            turned = turned + pltpu.roll(turned, step, 1)
        early = jnp.sum(jnp.where(row == lane // 16, turned, 0.0), axis=0, keepdims=True)
        late = jnp.sum(jnp.where(row == 8 + lax.rem(lane // 16, 4), turned, 0.0), axis=0, keepdims=True)
        o_ref[NB + 8 + 12 + 16 * n : NB + 9 + 12 + 16 * n, :] = early.astype(jnp.int32)
        o_ref[NB + 9 + 12 + 16 * n : NB + 10 + 12 + 16 * n, :] = late.astype(jnp.int32)


def up_setup(slot, slot_col, tables, group):
    theta, phi = lax.axis_index("theta"), lax.axis_index("phi")
    i0, k0 = theta * T2, phi * F2
    fill_phases(slot, tables, 136, i0 + k0 - 13, k0 - i0 - 34, i0 - 5, ROWS, PH2)
    parent = lax.rem(slot_col, 16)
    lane = iota((NB, NB), 1)
    for j in range(8):
        block = flags(lane == parent + 16 * j)
        group[j, 0:NB, :] = block
        group[j, NB : 2 * NB, :] = block


def up_rows(low, high, tile, slot_first, weight_ref, x_ref, up_ref, z_ref, rhs, lhs, group, tables):
    plus_c, plus_s, minus_c, minus_s, polar_c, polar_s = tables
    left = iota((8, NB), 0) >= 3

    def columns(table, start):
        main = table[pl.ds(start + 8, F2), :]
        edge = jnp.where(left, table[pl.ds(start, 8), :], table[pl.ds(start + 97, 8), :])
        return jnp.concatenate([main, edge], axis=0)

    def row(r, carry):
        base = (12 * (r - 5) - 5 + 110) // 22 - 5 - 2
        taps = [jnp.minimum(jnp.maximum(base + m, 0), T1 - 1) for m in range(6)]
        weights = [weight_ref[r * 6 + m] for m in range(6)]
        for c in range(8):
            y = weights[0] * x_ref[c, taps[0]]
            for m in range(1, 6):
                y = y + weights[m] * x_ref[c, taps[m]]
            hi, lo = halves(y)
            cut = slice(c * NB, c * NB + NB)
            rhs[0:F1, cut] = hi
            rhs[F1 : 2 * F1, cut] = lo
            rhs[2 * F1 : 3 * F1, cut] = hi
        v = jnp.dot(up_ref[...], rhs[...], preferred_element_type=F32)
        er, ei = times(
            columns(plus_c, r), columns(plus_s, r), columns(minus_c, 31 - r), columns(minus_s, 31 - r)
        )
        er, ei = times(er, ei, polar_c[pl.ds(r, 1), :], polar_s[pl.ds(r, 1), :])
        for c in range(4):
            vr, vi = v[:, c * NB : c * NB + NB], v[:, (c + 4) * NB : (c + 5) * NB]
            both = times(vr, vi, er, ei)
            for h in range(2):
                hi, lo = halves(both[h])
                cut = slice((c + 4 * h) * QX, (c + 4 * h + 1) * QX)
                lhs[cut, 0:NB] = hi
                lhs[cut, NB : 2 * NB] = lo
        summed = jnp.dot(lhs[...], group[r - low + slot_first], preferred_element_type=F32)
        z_ref[tile] = z_ref[tile] + summed.reshape(8, QX, NB)
        return carry

    lax.fori_loop(low, high, row, 0)


def neighbours():
    theta, phi = lax.axis_index("theta"), lax.axis_index("phi")
    last = lax.axis_size("theta") - 1
    ring = lax.axis_size("phi")
    right = lax.rem(phi + 1, ring)
    left = lax.rem(phi + ring - 1, ring)
    out = []
    for dt in (-1, 0, 1):
        for df, column in ((-1, left), (0, phi), (1, right)):
            if dt == 0 and df == 0:
                continue
            has = None if dt == 0 else (theta > 0 if dt < 0 else theta < last)
            out.append((dt, df, has, (theta + dt, column)))
    return out


def guarded(has, do):
    if has is None:
        do()
    else:
        pl.when(has)(do)


def greet(around):
    barrier = pltpu.get_barrier_semaphore()
    for dt, df, has, device in around:
        def signal(device=device):
            pl.semaphore_signal(barrier, inc=1, device_id=device, device_id_type=MESH)

        guarded(has, signal)


def met(around):
    barrier = pltpu.get_barrier_semaphore()
    inside = around[0][2] & around[-1][2]

    @pl.when(inside)
    def _():
        pl.semaphore_wait(barrier, 8)

    @pl.when(jnp.logical_not(inside))
    def _():
        pl.semaphore_wait(barrier, 5)


def exchange(around, wanted, source, landing, send_sem, recv_sem):
    for n, (dt, df, has, device) in enumerate(around):
        if wanted(dt):
            copy = pltpu.make_async_remote_copy(
                src_ref=source(dt, df),
                dst_ref=landing[(-dt, -df)],
                send_sem=send_sem.at[n],
                recv_sem=recv_sem.at[7 - n],
                device_id=device,
                device_id_type=MESH,
            )
            guarded(has, copy.start)


def finish(around, source, landing, send_sem, recv_sem):
    for n, (dt, df, has, device) in enumerate(around):
        copy = pltpu.make_async_remote_copy(
            src_ref=source(dt, df),
            dst_ref=landing[(dt, df)],
            send_sem=send_sem.at[n],
            recv_sem=recv_sem.at[n],
            device_id=device,
            device_id_type=MESH,
        )
        guarded(has, copy.wait)


STEP = 96


def child_setup(src_ref, kind_ref, hot_s, hot_k):
    row = lax.rem(iota((2 * NB, NB), 0), NB)
    for l in range(LIST):
        cut = slice(l * NB, l * NB + NB)
        hot_s[:, cut] = flags(row == src_ref[l : l + 1, :])
        hot_k[:, cut] = flags(row == kind_ref[l : l + 1, :])


def child_steps(low, high, x_ref, t_ref, o_ref, hot_s, hot_k, lx, lt):
    def step(g, carry):
        cut = pl.ds(2 * g, 2)
        for c in range(8):
            hi, lo = halves(x_ref[c, cut].reshape(STEP, NB))
            lx[c * STEP : (c + 1) * STEP, 0:NB] = hi
            lx[c * STEP : (c + 1) * STEP, NB : 2 * NB] = lo
        for c in range(2):
            hi, lo = halves(t_ref[c, cut].reshape(STEP, NB))
            lt[c * STEP : (c + 1) * STEP, 0:NB] = hi
            lt[c * STEP : (c + 1) * STEP, NB : 2 * NB] = lo
        total = [None] * 8
        for pair in range(LIST // 2):
            both = slice(pair * 2 * NB, (pair + 1) * 2 * NB)
            tt = jnp.dot(lt[...], hot_k[:, both], preferred_element_type=F32)
            xx = jnp.dot(lx[...], hot_s[:, both], preferred_element_type=F32)
            for h in range(2):
                one = slice(h * NB, h * NB + NB)
                a, b = tt[:STEP, one], tt[STEP:, one]
                for c in range(4):
                    u = xx[c * STEP : (c + 1) * STEP, one]
                    v = xx[(c + 4) * STEP : (c + 5) * STEP, one]
                    re, im = times(u, v, a, b)
                    total[c] = re if total[c] is None else total[c] + re
                    total[c + 4] = im if total[c + 4] is None else total[c + 4] + im
        for c in range(8):
            o_ref[c, cut] = total[c].reshape(2, F1, NB)
        return carry

    lax.fori_loop(low, high, step, 0)


def up_source(z_ref):
    def source(dt, df):
        if dt == 0:
            return z_ref.at[0:3, :, F2:QX, :]
        tile = 3 if dt < 0 else 4
        return z_ref.at[tile, :, 0:F2, :] if df == 0 else z_ref.at[tile, :, F2:QX, :]

    return source


def up_join(around, z_ref, landing):
    sub = iota((8, NB), 0)

    def from_left(tile, block):
        z_ref[tile, :, 0:8, :] += jnp.where((sub >= 1) & (sub <= 3), pltpu.roll(block, 1, 1), 0.0)

    def from_right(tile, block):
        z_ref[tile, :, F2 - 8 : F2, :] += jnp.where(sub >= 3, block, 0.0)

    for tile in range(3):
        from_left(tile, landing[(0, -1)][tile])
        from_right(tile, landing[(0, 1)][tile])

    @pl.when(around[0][2])
    def _():
        z_ref[0, :, 0:F2, :] += landing[(-1, 0)][...]
        from_left(0, landing[(-1, -1)][...])
        from_right(0, landing[(-1, 1)][...])

    @pl.when(around[-1][2])
    def _():
        z_ref[2, :, 0:F2, :] += landing[(1, 0)][...]
        from_left(2, landing[(1, -1)][...])
        from_right(2, landing[(1, 1)][...])


PAIRS = T2 // 2


def parent_setup(src_ref, kind_ref, hot_x, hot_a, hot_c, gather, inner, rd):
    lane = iota((NB, NB), 1)
    row = iota((NB, NB), 0)
    for half in range(2):
        cut = slice(half * NB, half * NB + NB)
        hot_a[cut, :] = flags(row == kind_ref[0:1, :])
        late = row == kind_ref[1:2, :]
        hot_c[0, cut, :] = flags(late & (lane < 64))
        hot_c[1, cut, :] = flags(late & (lane >= 64))
        for jj in range(4):
            hot_x[jj, cut, 0:NB] = flags(row == src_ref[0:1, :] + 32 * jj)
            hot_x[jj, cut, NB : 2 * NB] = flags(row == src_ref[0:1, :] + (32 * jj + 16))
            hot_x[jj, cut, 2 * NB : 3 * NB] = flags(row == src_ref[1:2, :] + (32 * jj + 16 * (lane // 64)))
    same = lax.rem(row, 16) == lax.rem(lane, 16)
    for jj in range(4):
        first = flags(same & (lane // 16 == 2 * jj))
        second = flags(same & (lane // 16 == 2 * jj + 1))
        third = flags(same & (lane // 16 == 2 * jj + row // 64))
        for half in range(2):
            gather[jj, half * NB : half * NB + NB, :] = first
            gather[jj, (2 + half) * NB : (3 + half) * NB, :] = second
            gather[jj, (4 + half) * NB : (5 + half) * NB, :] = third
    inner[...] = jnp.zeros_like(inner)
    rd[...] = jnp.zeros_like(rd)


def parent_rows(z_ref, t_ref, hot_x, hot_a, hot_c, gather, lx, lt, lp, inner):
    for tile in range(3):
        for c in range(8):
            hi, lo = halves(z_ref[tile, c, 0:F2, :])
            lx[tile, c * F2 : (c + 1) * F2, 0:NB] = hi
            lx[tile, c * F2 : (c + 1) * F2, NB : 2 * NB] = lo

    def pair(n, carry):
        tile, jj = n // 4, lax.rem(n, 4)
        for r in range(2):
            for c in range(2):
                hi, lo = halves(t_ref[c, 2 * n + r])
                lt[r, c * F2 : (c + 1) * F2, 0:NB] = hi
                lt[r, c * F2 : (c + 1) * F2, NB : 2 * NB] = lo
        tt = [
            jnp.dot(lt[0], hot_a[...], preferred_element_type=F32),
            jnp.dot(lt[1], hot_a[...], preferred_element_type=F32),
            jnp.dot(lt[0], hot_c[0], preferred_element_type=F32)
            + jnp.dot(lt[1], hot_c[1], preferred_element_type=F32),
        ]
        xx = jnp.dot(lx[tile], hot_x[jj], preferred_element_type=F32)
        for k in range(3):
            one = slice(k * NB, k * NB + NB)
            a, b = tt[k][:F2], tt[k][F2:]
            for c in range(4):
                u = xx[c * F2 : (c + 1) * F2, one]
                v = xx[(c + 4) * F2 : (c + 5) * F2, one]
                both = times(u, v, a, b)
                for h in range(2):
                    hi, lo = halves(both[h])
                    rows = slice((c + 4 * h) * F2, (c + 4 * h + 1) * F2)
                    lp[rows, 2 * k * NB : (2 * k + 1) * NB] = hi
                    lp[rows, (2 * k + 1) * NB : (2 * k + 2) * NB] = lo
        inner[tile] = inner[tile] + jnp.dot(lp[...], gather[jj], preferred_element_type=F32)
        return carry

    lax.fori_loop(0, PAIRS, pair, 0)


def parent_down(inner, theta_ref, phi_ref, w_ref, ld, rd):
    for tile in range(3):
        hi, lo = halves(inner[tile])
        ld[:, (3 * tile) * NB : (3 * tile + 1) * NB] = hi
        ld[:, (3 * tile + 1) * NB : (3 * tile + 2) * NB] = lo
        ld[:, (3 * tile + 2) * NB : (3 * tile + 3) * NB] = hi
    down = jnp.dot(ld[...], theta_ref[...], preferred_element_type=F32)
    for c in range(8):
        hi, lo = halves(down[c * F2 : (c + 1) * F2, :])
        cut = slice(c * 3 * NB, (c + 1) * 3 * NB)
        rd[0:F2, cut] = hi
        rd[96 : 96 + F2, cut] = lo
        rd[192 : 192 + F2, cut] = hi
    for c in range(8):
        cut = slice(c * 3 * NB, (c + 1) * 3 * NB)
        w_ref[c] = jnp.dot(phi_ref[...], rd[:, cut], preferred_element_type=F32)


def down_source(w_ref):
    def source(dt, df):
        rows = slice(0, F1) if df == 0 else slice(F1, 56)
        lanes = slice(0, 2 * NB) if dt == 0 else slice(2 * NB, 3 * NB)
        return w_ref.at[:, rows, lanes]

    return source


def down_join(around, w_ref, wo_ref, landing):
    wo_ref[...] = w_ref[:, 0:F1, 0 : 2 * NB]
    sub = iota((8, 2 * NB), 0)
    wo_ref[:, 0:8, :] += jnp.where(sub < 3, landing[(0, -1)][...], 0.0)
    wo_ref[:, F1 - 8 : F1, :] += jnp.where(sub >= 5, landing[(0, 1)][...], 0.0)
    lane = iota((F1, NB), 1)
    sub8, lane8 = iota((8, NB), 0), iota((8, NB), 1)

    @pl.when(around[0][2])
    def _():
        cut = slice(0, NB)
        wo_ref[:, :, cut] += jnp.where(lane < 48, landing[(-1, 0)][...], 0.0)
        wo_ref[:, 0:8, cut] += jnp.where((lane8 < 48) & (sub8 < 3), landing[(-1, -1)][...], 0.0)
        wo_ref[:, F1 - 8 : F1, cut] += jnp.where((lane8 < 48) & (sub8 >= 5), landing[(-1, 1)][...], 0.0)

    @pl.when(around[-1][2])
    def _():
        cut = slice(NB, 2 * NB)
        keep, keep8 = (lane >= 16) & (lane < 64), (lane8 >= 16) & (lane8 < 64)
        wo_ref[:, :, cut] += jnp.where(keep, pltpu.roll(landing[(1, 0)][...], 64, 2), 0.0)
        wo_ref[:, 0:8, cut] += jnp.where(keep8 & (sub8 < 3), pltpu.roll(landing[(1, -1)][...], 64, 2), 0.0)
        wo_ref[:, F1 - 8 : F1, cut] += jnp.where(keep8 & (sub8 >= 5), pltpu.roll(landing[(1, 1)][...], 64, 2), 0.0)


EARLY = 2


def main_kernel(weight_ref, index_ref, x_ref, tc_ref, tp_ref, up_ref, theta_ref, phi_ref, wo_ref, local_ref, *scratch):
    up_land, down_land, up_sems, down_sems = scratch[0:8], scratch[8:16], scratch[16:18], scratch[18:20]
    z_ref, rhs, lhs, group = scratch[20:24]
    tables = scratch[24:30]
    hot_s, hot_k, lx, lt = scratch[30:34]
    hot_x, hot_a, hot_c, gather, plx, plt, lp, inner, ld, rd, w_ref = scratch[34:45]
    keys = [(-1, 0), (1, 0), (0, -1), (0, 1), (-1, -1), (-1, 1), (1, -1), (1, 1)]
    up_landing, down_landing = dict(zip(keys, up_land)), dict(zip(keys, down_land))
    around = neighbours()
    greet(around)
    up_setup(index_ref[NB : NB + 1, :], index_ref[0:NB, :], tables, group)
    z_ref[...] = jnp.zeros_like(z_ref)
    shared = (weight_ref, x_ref, up_ref, z_ref, rhs, lhs, group, tables)
    up_rows(0, 5, 3, 1, *shared)
    up_rows(27, 32, 4, 0, *shared)
    child_setup(index_ref.at[NB + 8 : NB + 24], index_ref.at[NB + 24 : NB + 40], hot_s, hot_k)
    met(around)
    source = up_source(z_ref)
    exchange(around, lambda dt: dt != 0, source, up_landing, *up_sems)
    up_rows(5, 13, 0, 0, *shared)
    up_rows(13, 21, 1, 0, *shared)
    up_rows(21, 27, 2, 0, *shared)
    parent_setup(index_ref.at[NB + 20 : NB + 22], index_ref.at[NB + 36 : NB + 38], hot_x, hot_a, hot_c, gather, inner, rd)
    exchange(around, lambda dt: dt == 0, source, up_landing, *up_sems)
    children = (x_ref, tc_ref, local_ref, hot_s, hot_k, lx, lt)
    child_steps(0, EARLY, *children)
    finish(around, source, up_landing, *up_sems)
    up_join(around, z_ref, up_landing)
    parent_rows(z_ref, tp_ref, hot_x, hot_a, hot_c, gather, plx, plt, lp, inner)
    parent_down(inner, theta_ref, phi_ref, w_ref, ld, rd)
    source = down_source(w_ref)
    exchange(around, lambda dt: True, source, down_landing, *down_sems)
    child_steps(EARLY, T1 // 2, *children)
    finish(around, source, down_landing, *down_sems)
    down_join(around, w_ref, wo_ref, down_landing)


def final_kernel(slot_ref, w_ref, local_ref, o_ref, lw, spread, *tables):
    theta, phi = lax.axis_index("theta"), lax.axis_index("phi")
    t0, f0 = theta * T1, phi * F1
    fill_phases(slot_ref[...], tables, 64, t0 + f0, f0 - t0 - 11, t0, 16, PH1)
    plus_c, plus_s, minus_c, minus_s, polar_c, polar_s = tables
    row = iota((NB, NB), 0)
    parent = lax.rem(jnp.broadcast_to(slot_ref[...], (NB, NB)), 16)
    for j in range(8):
        block = flags(row == parent + 16 * j)
        spread[j, 0:NB, :] = block
        spread[j, NB : 2 * NB, :] = block
    for tile in range(2):
        for c in range(8):
            hi, lo = halves(w_ref[c, :, tile * NB : (tile + 1) * NB])
            lw[tile, c * F1 : (c + 1) * F1, 0:NB] = hi
            lw[tile, c * F1 : (c + 1) * F1, NB : 2 * NB] = lo

    def one_row(t, carry):
        wide = jnp.dot(lw[t // 8], spread[lax.rem(t, 8)], preferred_element_type=F32)
        er, ei = times(
            plus_c[pl.ds(t, F1), :],
            plus_s[pl.ds(t, F1), :],
            minus_c[pl.ds(11 - t, F1), :],
            minus_s[pl.ds(11 - t, F1), :],
        )
        er, ei = times(er, ei, polar_c[pl.ds(t, 1), :], polar_s[pl.ds(t, 1), :])
        for c in range(4):
            u, v = wide[c * F1 : (c + 1) * F1], wide[(c + 4) * F1 : (c + 5) * F1]
            re, im = times(u, v, er, -ei)
            o_ref[c, t] = re + local_ref[c, t]
            o_ref[c + 4, t] = im + local_ref[c + 4, t]
        return carry

    lax.fori_loop(0, T1, one_row, 0)


def phase_scratch(rows, polar_rows):
    return [pltpu.VMEM((rows, NB), F32)] * 4 + [pltpu.VMEM((polar_rows, NB), F32)] * 2


def shape(*dims):
    return jax.ShapeDtypeStruct(dims, F32)


def landing_scratch(column, row, corner):
    return [pltpu.VMEM(column, F32)] * 2 + [pltpu.VMEM(row, F32)] * 2 + [pltpu.VMEM(corner, F32)] * 4


def per_device(child_out, child_slot, sources_child, kinds_child, table_child, sources_parent, kinds_parent, table_parent):
    slot_row = child_slot.reshape(1, NB)
    params = dict(vmem_limit_bytes=60 * 1024 * 1024)
    index = pl.pallas_call(
        index_kernel,
        out_shape=jax.ShapeDtypeStruct((INDEX_ROWS, NB), jnp.int32),
        in_specs=[VM] * 5,
        out_specs=VM,
        scratch_shapes=[pltpu.VMEM((NB, NB), jnp.int32)],
        name="index",
    )(slot_row, sources_child, kinds_child, sources_parent, kinds_parent)

    wo, local = pl.pallas_call(
        main_kernel,
        out_shape=(shape(8, F1, 2 * NB), shape(8, T1, F1, NB)),
        in_specs=[SM] + [VM] * 7,
        out_specs=(VM, VM),
        scratch_shapes=landing_scratch((8, F2, NB), (3, 8, 8, NB), (8, 8, NB))
        + landing_scratch((8, F1, NB), (8, 8, 2 * NB), (8, 8, NB))
        + [pltpu.SemaphoreType.DMA((8,))] * 4
        + [
            pltpu.VMEM((5, 8, QX, NB), F32),
            pltpu.VMEM((3 * F1, 8 * NB), BF16),
            pltpu.VMEM((8 * QX, 2 * NB), BF16),
            pltpu.VMEM((8, 2 * NB, NB), BF16),
        ]
        + phase_scratch(136, ROWS)
        + [pltpu.VMEM((2 * NB, LIST * NB), BF16)] * 2
        + [pltpu.VMEM((8 * STEP, 2 * NB), BF16), pltpu.VMEM((2 * STEP, 2 * NB), BF16)]
        + [
            pltpu.VMEM((4, 2 * NB, 3 * NB), BF16),
            pltpu.VMEM((2 * NB, NB), BF16),
            pltpu.VMEM((2, 2 * NB, NB), BF16),
            pltpu.VMEM((4, 6 * NB, NB), BF16),
            pltpu.VMEM((3, 8 * F2, 2 * NB), BF16),
            pltpu.VMEM((2, 2 * F2, 2 * NB), BF16),
            pltpu.VMEM((8 * F2, 6 * NB), BF16),
            pltpu.VMEM((3, 8 * F2, NB), F32),
            pltpu.VMEM((8 * F2, 9 * NB), BF16),
            pltpu.VMEM((288, 8 * 3 * NB), BF16),
            pltpu.VMEM((8, 56, 3 * NB), F32),
        ],
        compiler_params=pltpu.CompilerParams(collective_id=0, has_side_effects=True, **params),
        name="main",
    )(
        jnp.asarray(theta_weights()),
        index,
        child_out,
        table_child,
        table_parent,
        jnp.asarray(phi_up()),
        jnp.asarray(theta_down()),
        jnp.asarray(phi_down()),
    )

    return pl.pallas_call(
        final_kernel,
        out_shape=shape(8, T1, F1, NB),
        in_specs=[VM] * 3,
        out_specs=VM,
        scratch_shapes=[pltpu.VMEM((2, 8 * F1, 2 * NB), BF16), pltpu.VMEM((8, 2 * NB, NB), BF16)]
        + phase_scratch(64, 16),
        compiler_params=pltpu.CompilerParams(**params),
        name="final",
    )(slot_row, wo, local)


def solution(mesh):
    block = P(None, "theta", "phi", None)
    return jax.shard_map(
        per_device,
        mesh=mesh,
        in_specs=(block, P(), P(), P(), block, P(), P(), block),
        out_specs=block,
        check_vma=False,
    )
```

time: 691 us -> 67.3 us (0.10); the launches traced: 680 us -> 67 us
  local copies, waits for them, and re-layouts: 375 us -> 2.83 us
  other arithmetic: 228 us -> 0 us
  Pallas kernels: 0 us -> 64.2 us
  waiting for transfers between devices: 29.3 us -> 0 us
  matrix products: 22.6 us -> 0 us
  starting transfers between devices: 22.1 us -> 0 us
    gather x50 -> x0, local copies, waits for them, and re-layouts: 175 us -> none  [the longest x24 90.5 us: accumulate(): gathered = jnp.take(pattern, source_column, axis=3)]
    add x25 -> x0, other arithmetic: 86.8 us -> none  [the longest x24 83.8 us: accumulate(): return (summed + complex_times(gathered, factor), None)]
    select_n x76 -> x0, other arithmetic: 79.7 us -> none  [the longest x48 52.2 us: accumulate(): gathered = jnp.take(pattern, source_column, axis=3)]
    pallas_call x0 -> x3, Pallas kernels: none -> 64.2 us  [the longest x1 55.7 us: per_device(): pl.pallas_call(main_kernel, out_shape=(shape(8, F1, 2 * NB), shape(8, T1,...]
    add x13 -> x0, local copies, waits for them, and re-layouts: 55.9 us -> none  [complex_times(): imag_out = halves[0] * sine_part + halves[1] * cosine]
    sub x25 -> x0, other arithmetic: 44.9 us -> none  [complex_times(): real_out = halves[0] * cosine - halves[1] * sine_part]
    slice x31 -> x0, local copies, waits for them, and re-layouts: 40 us -> none  [the longest x3 18.1 us: aggregate(): real_out = jnp.sum(halves[0] * cosine - halves[1] * sine_part, axis=3)]
    sub x13 -> x0, local copies, waits for them, and re-layouts: 32.3 us -> none  [complex_times(): real_out = halves[0] * cosine - halves[1] * sine_part]
  transfers between devices with their start and end apart: 8 -> 0, of which waited for: 4 -> 0; matrix products, arithmetic and copies ran while one was open for 61% -> 0% of each run, Pallas kernels for 0% -> 0%
where the time goes in v1:
time: 67.3 us; the launch traced here: 67 us
  Pallas kernels  64.2 us (95%)
  local copies, waits for them, and re-layouts  2.83 us (4%)
    pallas_call x1, Pallas kernels, per_device(): pl.pallas_call(main_kernel, out_shape=(shape(8, F1, 2 * NB), shape(8, T1,...  55.7 us
    pallas_call x1, Pallas kernels, per_device(): pl.pallas_call(final_kernel, out_shape=shape(8, T1, F1, NB), in_specs=[VM...  6.53 us
    unnamed x2, local copies, waits for them, and re-layouts  2.83 us
    pallas_call x1, Pallas kernels, per_device(): pl.pallas_call(index_kernel, out_shape=jax.ShapeDtypeStruct((INDEX_ROWS,...  1.87 us

profile of v1, /device:TPU:3, one launch (start us, length us, event | category | flops | bytes accessed | tf_op | source)
XLA Modules:
  0.0 67.0 jit_solution(13366305509684943470)
XLA Ops:
  0.0 1.4 %copy.13.sc_ref = s32[128,12]{1,0:T(8,128)} copy(s32[128,12]{0,1:T(8,128)} %param.14) | data formatting | bytes 12288 | tf_op args[2]
  1.4 1.4 %copy.14.kc_ref = s32[128,12]{1,0:T(8,128)} copy(s32[128,12]{0,1:T(8,128)} %param.15) | data formatting | bytes 12288 | tf_op args[3]
  2.8 1.9 %index.1.index_ref = s32[168,128]{1,0:T(8,128)} custom-call(s32[1,128]{1,0:T(1,128)} %bitcast.1, s32[128,12]{1,0:T(8,128)} %copy.13.sc_ref, s32[128,12]{1,0:T(8,128)} %copy.14.kc_ref, s32[16,12]{1,0:T(8,128)} %sp_ref.1, s32[16,12]{1,0:T(8,128)} %kp_ref.1), custom_call_target="tpu_custom_call" | custom-call | tf_op jit(solution)/shard_map/index/pallas_call | solution.py:601
  4.7 55.7 %main.1 = (f32[8,48,256]{2,1,0:T(8,128)}, f32[8,12,48,128]{3,2,1,0:T(8,128)}) custom-call(f32[192]{0:T(256)} %constant.8.clone.weight_ref, s32[168,128]{1,0:T(8,128)} %index.1.index_ref, f32[8,12,48,128]{3,2,1,0:T(8,128)} %x_ref.1, f32[2,12,48,128]{3,2,1,0:T(8,128)} %tc_ref.1, f32[2,22,88,128]{3,2,1,0:T(8,128)} %tp_ref.1, ...), custom_call_target="tpu_custom_call" | custom-call | tf_op jit(solution)/shard_map/main/pallas_call | solution.py:610
  60.5 6.5 %final.1 = f32[8,12,48,128]{3,2,1,0:T(8,128)} custom-call(s32[1,128]{1,0:T(1,128)} %bitcast.2, f32[8,48,256]{2,1,0:T(8,128)} %get-tuple-element.7.w_ref, f32[8,12,48,128]{3,2,1,0:T(8,128)} %get-tuple-element.8.local_ref), custom_call_target="tpu_custom_call" | custom-call | tf_op jit(solution)/shard_map/final/pallas_call | solution.py:653

commit v2 on v1

--- a/solution.py
+++ b/solution.py
@@ -15,12 +15,13 @@
 T1, F1, T2, F2 = 12, 48, 22, 88
 QX = 96
 NB = 128
-ROWS = 32
+ROWS = 34
 WAVE = BAND1 / (2.0 * math.sqrt(3.0))
+REVERSED = (0, 4, 2, 6, 1, 5, 3, 7)
 F32, BF16 = jnp.float32, jnp.bfloat16
 MESH = pl.DeviceIdType.MESH
 VM = pl.BlockSpec(memory_space=pltpu.VMEM)
-SM = pl.BlockSpec(memory_space=pltpu.SMEM)
+ANY = pl.BlockSpec(memory_space=pl.ANY)
 
 
 def stencil(count_out, count_in, centered, row_out):
@@ -56,13 +57,24 @@
     return list(range(F1)) + [48, 49, 50, None, None, -3, -2, -1]
 
 
-def theta_weights():
-    weight = np.zeros((ROWS * 6,), np.float32)
-    for r in range(ROWS):
-        base, weights = stencil(TH2, TH1, True, r - 5)
+def theta_up(first, last, t_first, t_last):
+    matrix = np.zeros((last - first, t_last - t_first))
+    for p in range(first, last):
+        base, weights = stencil(TH2, TH1, True, p)
         for m in range(6):
-            weight[r * 6 + m] = weights[m] if 0 <= base - 2 + m < T1 else 0.0
-    return weight
+            t = base - 2 + m
+            if 0 <= t < T1:
+                matrix[p - first, t - t_first] += weights[m]
+    high, low = as_halves(np.kron(matrix, np.eye(8)))
+    return np.concatenate([high, high, low], axis=1)
+
+
+BLOCKS = (
+    (-6, 0, 0, 4, ((3, -6),)),
+    (22, 28, 8, 12, ((4, 22),)),
+    (0, 8, 0, 8, ((0, 0),)),
+    (8, 22, 2, 12, ((1, 8), (2, 16))),
+)
 
 
 def phi_up():
@@ -101,6 +113,7 @@
         base, weights = stencil(TH2, TH1, True, p)
         for m in range(6):
             matrix[p, slots[base - 2 + m]] += weights[m]
+    matrix = matrix[[8 * (g // 8) + REVERSED[g % 8] for g in range(24)]]
     big = np.kron(matrix, np.eye(16))
     high, low = as_halves(big)
     parts = []
@@ -167,10 +180,8 @@
     o_ref[0:NB, :] = jnp.broadcast_to(slot_ref[...], (NB, NB)).T
     o_ref[NB : NB + 8, :] = jnp.broadcast_to(slot_ref[...], (8, NB))
     lane, row = iota((16, NB), 1), iota((16, NB), 0)
-    wide[...] = jnp.zeros_like(wide)
     for n, ref in enumerate((sc_ref, kc_ref)):
-        wide[:, 0:LIST] = ref[...]
-        o_ref[NB + 8 + 16 * n : NB + 24 + 16 * n, :] = wide[...].T[0:16]
+        o_ref[NB + 8 + 16 * n : NB + 8 + LIST + 16 * n, :] = ref[...]
     wide[...] = jnp.zeros_like(wide)
     for n, ref in enumerate((sp_ref, kp_ref)):
         wide[0:16, 0:LIST] = ref[...]
@@ -183,19 +194,44 @@
         o_ref[NB + 9 + 12 + 16 * n : NB + 10 + 12 + 16 * n, :] = late.astype(jnp.int32)
 
 
-def up_setup(slot, slot_col, tables, group):
+def first_of_pair(m):
+    lane = lax.rem(iota((1, NB), 1) + (128 - 32 * lax.rem(m, 2) - 16 * (m // 2)), 128)
+    return lane < 64
+
+
+def merge(keep, a, b, shift):
+    return jnp.where(keep, a, b) + pltpu.roll(jnp.where(keep, b, a), shift, 1)
+
+
+def merge_tile(pairs, count):
+    lane = iota((1, NB), 1)
+    first, second = lax.rem(lane, 64) < 32, lax.rem(lane + 112, 64) < 32
+    even = lax.rem(lane, 32) < 16
+    late = pairs[3] if count == 4 else jnp.zeros_like(pairs[2])
+    return merge(even, merge(first, pairs[0], pairs[1], 96), merge(second, pairs[2], late, 96), 112)
+
+
+def up_setup(slot_col, load_x, x_ref, up_ref, lhs, order, xh, xl, vh, vl, er_ref, ei_ref, tables):
     theta, phi = lax.axis_index("theta"), lax.axis_index("phi")
     i0, k0 = theta * T2, phi * F2
-    fill_phases(slot, tables, 136, i0 + k0 - 13, k0 - i0 - 34, i0 - 5, ROWS, PH2)
-    parent = lax.rem(slot_col, 16)
-    lane = iota((NB, NB), 1)
-    for j in range(8):
-        block = flags(lane == parent + 16 * j)
-        group[j, 0:NB, :] = block
-        group[j, NB : 2 * NB, :] = block
-
-
-def up_rows(low, high, tile, slot_first, weight_ref, x_ref, up_ref, z_ref, rhs, lhs, group, tables):
+    fill_phases(iota((1, NB), 1), tables, 144, i0 + k0 - 14, k0 - i0 - 35, i0 - 6, 40, PH2)
+    block = flags(iota((NB, NB), 1) == slot_col)
+    order[...] = jnp.zeros_like(order)
+    order[0:NB, 0:NB] = block
+    order[NB : 2 * NB, NB : 2 * NB] = block
+
+    load_x.wait()
+
+    def turn(c, carry):
+        hi, lo = halves(x_ref[c].reshape(T1 * F1, NB))
+        lhs[:, 0:NB] = hi
+        lhs[:, NB : 2 * NB] = lo
+        out = jnp.dot(lhs[...], order[...], preferred_element_type=F32)
+        xh[c] = out[:, 0:NB].astype(BF16).reshape(T1, F1, NB)
+        xl[c] = out[:, NB : 2 * NB].astype(BF16).reshape(T1, F1, NB)
+        return carry
+
+    lax.fori_loop(0, 8, turn, 0)
     plus_c, plus_s, minus_c, minus_s, polar_c, polar_s = tables
     left = iota((8, NB), 0) >= 3
 
@@ -204,37 +240,60 @@
         edge = jnp.where(left, table[pl.ds(start, 8), :], table[pl.ds(start + 97, 8), :])
         return jnp.concatenate([main, edge], axis=0)
 
-    def row(r, carry):
-        base = (12 * (r - 5) - 5 + 110) // 22 - 5 - 2
-        taps = [jnp.minimum(jnp.maximum(base + m, 0), T1 - 1) for m in range(6)]
-        weights = [weight_ref[r * 6 + m] for m in range(6)]
-        for c in range(8):
-            y = weights[0] * x_ref[c, taps[0]]
-            for m in range(1, 6):
-                y = y + weights[m] * x_ref[c, taps[m]]
-            hi, lo = halves(y)
-            cut = slice(c * NB, c * NB + NB)
-            rhs[0:F1, cut] = hi
-            rhs[F1 : 2 * F1, cut] = lo
-            rhs[2 * F1 : 3 * F1, cut] = hi
-        v = jnp.dot(up_ref[...], rhs[...], preferred_element_type=F32)
-        er, ei = times(
-            columns(plus_c, r), columns(plus_s, r), columns(minus_c, 31 - r), columns(minus_s, 31 - r)
-        )
-        er, ei = times(er, ei, polar_c[pl.ds(r, 1), :], polar_s[pl.ds(r, 1), :])
+    def two_rows(n, carry):
         for c in range(4):
-            vr, vi = v[:, c * NB : c * NB + NB], v[:, (c + 4) * NB : (c + 5) * NB]
-            both = times(vr, vi, er, ei)
+            outs = []
             for h in range(2):
-                hi, lo = halves(both[h])
-                cut = slice((c + 4 * h) * QX, (c + 4 * h + 1) * QX)
-                lhs[cut, 0:NB] = hi
-                lhs[cut, NB : 2 * NB] = lo
-        summed = jnp.dot(lhs[...], group[r - low + slot_first], preferred_element_type=F32)
-        z_ref[tile] = z_ref[tile] + summed.reshape(8, QX, NB)
+                t = 2 * n + h
+                high = jnp.concatenate([xh[c, t], xh[c + 4, t]], axis=1)
+                low = jnp.concatenate([xl[c, t], xl[c + 4, t]], axis=1)
+                rhs = jnp.concatenate([high, low, high], axis=0)
+                outs.append(jnp.dot(up_ref[...], rhs, preferred_element_type=F32))
+            at = pl.ds(pl.multiple_of(16 * n, 16), 16)
+            for g in range(12):
+                rows = slice(8 * g, 8 * g + 8)
+                hi, lo = halves(jnp.concatenate([outs[0][rows], outs[1][rows]], axis=0))
+                vh[g, c, at, :] = hi
+                vl[g, c, at, :] = lo
+        for extra in range(6):
+            r = jnp.minimum(6 * n + extra, ROWS - 1)
+            e = times(columns(plus_c, r), columns(plus_s, r), columns(minus_c, 33 - r), columns(minus_s, 33 - r))
+            e = times(*e, polar_c[pl.ds(r, 1), :], polar_s[pl.ds(r, 1), :])
+            er_ref[r], ei_ref[r] = e
         return carry
 
-    lax.fori_loop(low, high, row, 0)
+    lax.fori_loop(0, 6, two_rows, 0)
+
+
+def up_blocks(numbers, theta_refs, z_ref, vh, vl, er_ref, ei_ref):
+    keeps = [first_of_pair(m) for m in range(4)]
+
+    def group(g, carry):
+        rows = pl.ds(pl.multiple_of(8 * g, 8), 8)
+        for number in numbers:
+            first, last, t_first, t_last, tiles = BLOCKS[number]
+            matrix = theta_refs[number]
+            for c in range(4):
+                part = slice(8 * t_first, 8 * t_last)
+                high = vh[g, c, part, :]
+                rhs = jnp.concatenate([high, vl[g, c, part, :], high], axis=0)
+                v = jnp.dot(matrix[...], rhs, preferred_element_type=F32)
+                for tile, start in tiles:
+                    count = min(8, last - start) // 2
+                    pairs = ([], [])
+                    for m in range(count):
+                        found = []
+                        for p in (start + 2 * m, start + 2 * m + 1):
+                            here = slice(8 * (p - first), 8 * (p - first) + 8)
+                            e = er_ref[p + 6, rows, :], ei_ref[p + 6, rows, :]
+                            found.append(times(v[here, 0:NB], v[here, NB : 2 * NB], *e))
+                        for h in range(2):
+                            pairs[h].append(merge(keeps[m], found[0][h], found[1][h], 64))
+                    for h in range(2):
+                        z_ref[tile, c + 4 * h, rows, :] = merge_tile(pairs[h], count)
+        return carry
+
+    lax.fori_loop(0, 12, group, 0)
 
 
 def neighbours():
@@ -391,33 +450,27 @@
 PAIRS = T2 // 2
 
 
-def parent_setup(src_ref, kind_ref, hot_x, hot_a, hot_c, gather, inner, rd):
-    lane = iota((NB, NB), 1)
+def parent_setup(src_ref, kind_ref, hot_x, hot_t, sums):
     row = iota((NB, NB), 0)
-    for half in range(2):
-        cut = slice(half * NB, half * NB + NB)
-        hot_a[cut, :] = flags(row == kind_ref[0:1, :])
+    for jj in range(4):
+        keep = first_of_pair(jj)
+        slot0, slot1 = REVERSED[2 * jj], REVERSED[2 * jj + 1]
+        late_slot = jnp.where(keep, 16 * slot0, 16 * slot1)
         late = row == kind_ref[1:2, :]
-        hot_c[0, cut, :] = flags(late & (lane < 64))
-        hot_c[1, cut, :] = flags(late & (lane >= 64))
-        for jj in range(4):
-            hot_x[jj, cut, 0:NB] = flags(row == src_ref[0:1, :] + 32 * jj)
-            hot_x[jj, cut, NB : 2 * NB] = flags(row == src_ref[0:1, :] + (32 * jj + 16))
-            hot_x[jj, cut, 2 * NB : 3 * NB] = flags(row == src_ref[1:2, :] + (32 * jj + 16 * (lane // 64)))
-    same = lax.rem(row, 16) == lax.rem(lane, 16)
-    for jj in range(4):
-        first = flags(same & (lane // 16 == 2 * jj))
-        second = flags(same & (lane // 16 == 2 * jj + 1))
-        third = flags(same & (lane // 16 == 2 * jj + row // 64))
         for half in range(2):
-            gather[jj, half * NB : half * NB + NB, :] = first
-            gather[jj, (2 + half) * NB : (3 + half) * NB, :] = second
-            gather[jj, (4 + half) * NB : (5 + half) * NB, :] = third
-    inner[...] = jnp.zeros_like(inner)
-    rd[...] = jnp.zeros_like(rd)
-
-
-def parent_rows(z_ref, t_ref, hot_x, hot_a, hot_c, gather, lx, lt, lp, inner):
+            cut = slice(half * NB, half * NB + NB)
+            hot_x[jj, cut, 0:NB] = flags(row == src_ref[0:1, :] + 16 * slot0)
+            hot_x[jj, cut, NB : 2 * NB] = flags(row == src_ref[0:1, :] + 16 * slot1)
+            hot_x[jj, cut, 2 * NB : 3 * NB] = flags(row == src_ref[1:2, :] + late_slot)
+            early = flags(row == kind_ref[0:1, :])
+            hot_t[jj, 0, cut, 0:NB] = early
+            hot_t[jj, 1, cut, 0:NB] = early
+            hot_t[jj, 0, cut, NB : 2 * NB] = flags(late & keep)
+            hot_t[jj, 1, cut, NB : 2 * NB] = flags(late & jnp.logical_not(keep))
+    sums[11] = jnp.zeros_like(sums[11])
+
+
+def parent_rows(z_ref, t_ref, hot_x, hot_t, lx, lt, sums):
     for tile in range(3):
         for c in range(8):
             hi, lo = halves(z_ref[tile, c, 0:F2, :])
@@ -426,39 +479,34 @@
 
     def pair(n, carry):
         tile, jj = n // 4, lax.rem(n, 4)
+        keep = first_of_pair(jj)
         for r in range(2):
             for c in range(2):
                 hi, lo = halves(t_ref[c, 2 * n + r])
                 lt[r, c * F2 : (c + 1) * F2, 0:NB] = hi
                 lt[r, c * F2 : (c + 1) * F2, NB : 2 * NB] = lo
-        tt = [
-            jnp.dot(lt[0], hot_a[...], preferred_element_type=F32),
-            jnp.dot(lt[1], hot_a[...], preferred_element_type=F32),
-            jnp.dot(lt[0], hot_c[0], preferred_element_type=F32)
-            + jnp.dot(lt[1], hot_c[1], preferred_element_type=F32),
-        ]
+        t0 = jnp.dot(lt[0], hot_t[jj, 0], preferred_element_type=F32)
+        t1 = jnp.dot(lt[1], hot_t[jj, 1], preferred_element_type=F32)
+        tt = [t0[:, 0:NB], t1[:, 0:NB], t0[:, NB : 2 * NB] + t1[:, NB : 2 * NB]]
         xx = jnp.dot(lx[tile], hot_x[jj], preferred_element_type=F32)
-        for k in range(3):
-            one = slice(k * NB, k * NB + NB)
-            a, b = tt[k][:F2], tt[k][F2:]
-            for c in range(4):
+        for c in range(4):
+            parts = []
+            for k in range(3):
+                one = slice(k * NB, k * NB + NB)
                 u = xx[c * F2 : (c + 1) * F2, one]
                 v = xx[(c + 4) * F2 : (c + 5) * F2, one]
-                both = times(u, v, a, b)
-                for h in range(2):
-                    hi, lo = halves(both[h])
-                    rows = slice((c + 4 * h) * F2, (c + 4 * h + 1) * F2)
-                    lp[rows, 2 * k * NB : (2 * k + 1) * NB] = hi
-                    lp[rows, (2 * k + 1) * NB : (2 * k + 2) * NB] = lo
-        inner[tile] = inner[tile] + jnp.dot(lp[...], gather[jj], preferred_element_type=F32)
+                parts.append(times(u, v, tt[k][:F2], tt[k][F2:]))
+            for h in range(2):
+                value = merge(keep, parts[0][h], parts[1][h], 64) + parts[2][h]
+                sums[n, (c + 4 * h) * F2 : (c + 4 * h + 1) * F2, :] = value
         return carry
 
     lax.fori_loop(0, PAIRS, pair, 0)
 
 
-def parent_down(inner, theta_ref, phi_ref, w_ref, ld, rd):
+def parent_down(sums, theta_ref, phi_ref, w_ref, ld, rd):
     for tile in range(3):
-        hi, lo = halves(inner[tile])
+        hi, lo = halves(merge_tile([sums[4 * tile + m] for m in range(4)], 4))
         ld[:, (3 * tile) * NB : (3 * tile + 1) * NB] = hi
         ld[:, (3 * tile + 1) * NB : (3 * tile + 2) * NB] = lo
         ld[:, (3 * tile + 2) * NB : (3 * tile + 3) * NB] = hi
@@ -474,11 +522,22 @@
         w_ref[c] = jnp.dot(phi_ref[...], rd[:, cut], preferred_element_type=F32)
 
 
-def down_source(w_ref):
+def down_pack(w_ref, send_up, send_down):
+    low = iota((F1 // 2, NB), 1) < 64
+    for c in range(8):
+        near = w_ref[c, 0 : F1 // 2, 2 * NB : 3 * NB]
+        far = pltpu.roll(w_ref[c, F1 // 2 : F1, 2 * NB : 3 * NB], 64, 1)
+        send_up[c] = jnp.where(low, near, far)
+        send_down[c] = jnp.where(low, far, near)
+
+
+def down_source(w_ref, send_up, send_down):
     def source(dt, df):
-        rows = slice(0, F1) if df == 0 else slice(F1, 56)
-        lanes = slice(0, 2 * NB) if dt == 0 else slice(2 * NB, 3 * NB)
-        return w_ref.at[:, rows, lanes]
+        if df == 0:
+            return send_up if dt > 0 else send_down
+        if dt == 0:
+            return w_ref.at[:, F1:56, 0 : 2 * NB]
+        return w_ref.at[:, F1:56, 2 * NB : 3 * NB]
 
     return source
 
@@ -488,13 +547,17 @@
     sub = iota((8, 2 * NB), 0)
     wo_ref[:, 0:8, :] += jnp.where(sub < 3, landing[(0, -1)][...], 0.0)
     wo_ref[:, F1 - 8 : F1, :] += jnp.where(sub >= 5, landing[(0, 1)][...], 0.0)
-    lane = iota((F1, NB), 1)
+    half = F1 // 2
+    lane = iota((half, NB), 1)
     sub8, lane8 = iota((8, NB), 0), iota((8, NB), 1)
 
     @pl.when(around[0][2])
     def _():
         cut = slice(0, NB)
-        wo_ref[:, :, cut] += jnp.where(lane < 48, landing[(-1, 0)][...], 0.0)
+        for c in range(8):
+            got = landing[(-1, 0)][c]
+            wo_ref[c, 0:half, cut] += jnp.where(lane < 48, got, 0.0)
+            wo_ref[c, half:F1, cut] += jnp.where(lane < 48, pltpu.roll(got, 64, 1), 0.0)
         wo_ref[:, 0:8, cut] += jnp.where((lane8 < 48) & (sub8 < 3), landing[(-1, -1)][...], 0.0)
         wo_ref[:, F1 - 8 : F1, cut] += jnp.where((lane8 < 48) & (sub8 >= 5), landing[(-1, 1)][...], 0.0)
 
@@ -502,7 +565,10 @@
     def _():
         cut = slice(NB, 2 * NB)
         keep, keep8 = (lane >= 16) & (lane < 64), (lane8 >= 16) & (lane8 < 64)
-        wo_ref[:, :, cut] += jnp.where(keep, pltpu.roll(landing[(1, 0)][...], 64, 2), 0.0)
+        for c in range(8):
+            got = landing[(1, 0)][c]
+            wo_ref[c, 0:half, cut] += jnp.where(keep, pltpu.roll(got, 64, 1), 0.0)
+            wo_ref[c, half:F1, cut] += jnp.where(keep, got, 0.0)
         wo_ref[:, 0:8, cut] += jnp.where(keep8 & (sub8 < 3), pltpu.roll(landing[(1, -1)][...], 64, 2), 0.0)
         wo_ref[:, F1 - 8 : F1, cut] += jnp.where(keep8 & (sub8 >= 5), pltpu.roll(landing[(1, 1)][...], 64, 2), 0.0)
 
@@ -510,61 +576,88 @@
 EARLY = 2
 
 
-def main_kernel(weight_ref, index_ref, x_ref, tc_ref, tp_ref, up_ref, theta_ref, phi_ref, wo_ref, local_ref, *scratch):
+def main_kernel(
+    index_ref, x_far, tc_far, tp_far, theta_far, up_ref, ta_ref, tb_ref, tc2_ref, td_ref, phi_ref, wo_ref, local_far, *scratch
+):
     up_land, down_land, up_sems, down_sems = scratch[0:8], scratch[8:16], scratch[16:18], scratch[18:20]
-    z_ref, rhs, lhs, group = scratch[20:24]
-    tables = scratch[24:30]
-    hot_s, hot_k, lx, lt = scratch[30:34]
-    hot_x, hot_a, hot_c, gather, plx, plt, lp, inner, ld, rd, w_ref = scratch[34:45]
+    z_ref, lhs, order, xh, xl, vh, vl, er_ref, ei_ref = scratch[20:29]
+    tables = scratch[29:35]
+    hot_s, hot_k, lx, lt = scratch[35:39]
+    hot_x, hot_t, plx, plt, sums, ld, rd, w_ref = scratch[39:47]
+    x_ref, tc_ref, tp_ref, theta_ref, local_ref, send_up, send_down, load_sem, store_sem = scratch[47:56]
+    loads = [
+        pltpu.make_async_copy(far, near, load_sem.at[n])
+        for n, (far, near) in enumerate(
+            ((x_far, x_ref), (tc_far, tc_ref), (tp_far, tp_ref), (theta_far, theta_ref))
+        )
+    ]
+    stores = [
+        pltpu.make_async_copy(local_ref.at[:, rows], local_far.at[:, rows], store_sem.at[n])
+        for n, rows in enumerate((slice(0, 2 * EARLY), slice(2 * EARLY, T1)))
+    ]
+    for load in loads:
+        load.start()
     keys = [(-1, 0), (1, 0), (0, -1), (0, 1), (-1, -1), (-1, 1), (1, -1), (1, 1)]
     up_landing, down_landing = dict(zip(keys, up_land)), dict(zip(keys, down_land))
     around = neighbours()
     greet(around)
-    up_setup(index_ref[NB : NB + 1, :], index_ref[0:NB, :], tables, group)
-    z_ref[...] = jnp.zeros_like(z_ref)
-    shared = (weight_ref, x_ref, up_ref, z_ref, rhs, lhs, group, tables)
-    up_rows(0, 5, 3, 1, *shared)
-    up_rows(27, 32, 4, 0, *shared)
+    up_setup(index_ref[0:NB, :], loads[0], x_ref, up_ref, lhs, order, xh, xl, vh, vl, er_ref, ei_ref, tables)
+    shared = ((ta_ref, tb_ref, tc2_ref, td_ref), z_ref, vh, vl, er_ref, ei_ref)
+    up_blocks((0, 1), *shared)
     child_setup(index_ref.at[NB + 8 : NB + 24], index_ref.at[NB + 24 : NB + 40], hot_s, hot_k)
     met(around)
     source = up_source(z_ref)
     exchange(around, lambda dt: dt != 0, source, up_landing, *up_sems)
-    up_rows(5, 13, 0, 0, *shared)
-    up_rows(13, 21, 1, 0, *shared)
-    up_rows(21, 27, 2, 0, *shared)
-    parent_setup(index_ref.at[NB + 20 : NB + 22], index_ref.at[NB + 36 : NB + 38], hot_x, hot_a, hot_c, gather, inner, rd)
+    up_blocks((2, 3), *shared)
+    rd[...] = jnp.zeros_like(rd)
+    parent_setup(index_ref.at[NB + 20 : NB + 22], index_ref.at[NB + 36 : NB + 38], hot_x, hot_t, sums)
     exchange(around, lambda dt: dt == 0, source, up_landing, *up_sems)
     children = (x_ref, tc_ref, local_ref, hot_s, hot_k, lx, lt)
+    loads[1].wait()
     child_steps(0, EARLY, *children)
+    stores[0].start()
     finish(around, source, up_landing, *up_sems)
     up_join(around, z_ref, up_landing)
-    parent_rows(z_ref, tp_ref, hot_x, hot_a, hot_c, gather, plx, plt, lp, inner)
-    parent_down(inner, theta_ref, phi_ref, w_ref, ld, rd)
-    source = down_source(w_ref)
+    loads[2].wait()
+    loads[3].wait()
+    parent_rows(z_ref, tp_ref, hot_x, hot_t, plx, plt, sums)
+    parent_down(sums, theta_ref, phi_ref, w_ref, ld, rd)
+    down_pack(w_ref, send_up, send_down)
+    source = down_source(w_ref, send_up, send_down)
     exchange(around, lambda dt: True, source, down_landing, *down_sems)
     child_steps(EARLY, T1 // 2, *children)
+    stores[1].start()
     finish(around, source, down_landing, *down_sems)
     down_join(around, w_ref, wo_ref, down_landing)
+    for store in stores:
+        store.wait()
+
+
+FINAL = 2
 
 
 def final_kernel(slot_ref, w_ref, local_ref, o_ref, lw, spread, *tables):
-    theta, phi = lax.axis_index("theta"), lax.axis_index("phi")
-    t0, f0 = theta * T1, phi * F1
-    fill_phases(slot_ref[...], tables, 64, t0 + f0, f0 - t0 - 11, t0, 16, PH1)
     plus_c, plus_s, minus_c, minus_s, polar_c, polar_s = tables
-    row = iota((NB, NB), 0)
-    parent = lax.rem(jnp.broadcast_to(slot_ref[...], (NB, NB)), 16)
-    for j in range(8):
-        block = flags(row == parent + 16 * j)
-        spread[j, 0:NB, :] = block
-        spread[j, NB : 2 * NB, :] = block
-    for tile in range(2):
-        for c in range(8):
-            hi, lo = halves(w_ref[c, :, tile * NB : (tile + 1) * NB])
-            lw[tile, c * F1 : (c + 1) * F1, 0:NB] = hi
-            lw[tile, c * F1 : (c + 1) * F1, NB : 2 * NB] = lo
-
-    def one_row(t, carry):
+
+    @pl.when(pl.program_id(0) == 0)
+    def _():
+        theta, phi = lax.axis_index("theta"), lax.axis_index("phi")
+        t0, f0 = theta * T1, phi * F1
+        fill_phases(slot_ref[...], tables, 64, t0 + f0, f0 - t0 - 11, t0, 16, PH1)
+        row = iota((NB, NB), 0)
+        parent = lax.rem(jnp.broadcast_to(slot_ref[...], (NB, NB)), 16)
+        for j in range(8):
+            block = flags(row == parent + 16 * j)
+            spread[j, 0:NB, :] = block
+            spread[j, NB : 2 * NB, :] = block
+        for tile in range(2):
+            for c in range(8):
+                hi, lo = halves(w_ref[c, :, tile * NB : (tile + 1) * NB])
+                lw[tile, c * F1 : (c + 1) * F1, 0:NB] = hi
+                lw[tile, c * F1 : (c + 1) * F1, NB : 2 * NB] = lo
+
+    for n in range(FINAL):
+        t = pl.program_id(0) * FINAL + n
         wide = jnp.dot(lw[t // 8], spread[lax.rem(t, 8)], preferred_element_type=F32)
         er, ei = times(
             plus_c[pl.ds(t, F1), :],
@@ -576,11 +669,8 @@
         for c in range(4):
             u, v = wide[c * F1 : (c + 1) * F1], wide[(c + 4) * F1 : (c + 5) * F1]
             re, im = times(u, v, er, -ei)
-            o_ref[c, t] = re + local_ref[c, t]
-            o_ref[c + 4, t] = im + local_ref[c + 4, t]
-        return carry
-
-    lax.fori_loop(0, T1, one_row, 0)
+            o_ref[c, n] = re + local_ref[c, n]
+            o_ref[c + 4, n] = im + local_ref[c + 4, n]
 
 
 def phase_scratch(rows, polar_rows):
@@ -605,56 +695,72 @@
         out_specs=VM,
         scratch_shapes=[pltpu.VMEM((NB, NB), jnp.int32)],
         name="index",
-    )(slot_row, sources_child, kinds_child, sources_parent, kinds_parent)
+    )(slot_row, sources_child.T, kinds_child.T, sources_parent, kinds_parent)
 
     wo, local = pl.pallas_call(
         main_kernel,
         out_shape=(shape(8, F1, 2 * NB), shape(8, T1, F1, NB)),
-        in_specs=[SM] + [VM] * 7,
-        out_specs=(VM, VM),
+        in_specs=[VM] + [ANY] * 4 + [VM] * 6,
+        out_specs=(VM, ANY),
         scratch_shapes=landing_scratch((8, F2, NB), (3, 8, 8, NB), (8, 8, NB))
-        + landing_scratch((8, F1, NB), (8, 8, 2 * NB), (8, 8, NB))
+        + landing_scratch((8, F1 // 2, NB), (8, 8, 2 * NB), (8, 8, NB))
         + [pltpu.SemaphoreType.DMA((8,))] * 4
         + [
             pltpu.VMEM((5, 8, QX, NB), F32),
-            pltpu.VMEM((3 * F1, 8 * NB), BF16),
-            pltpu.VMEM((8 * QX, 2 * NB), BF16),
-            pltpu.VMEM((8, 2 * NB, NB), BF16),
+            pltpu.VMEM((T1 * F1, 2 * NB), BF16),
+            pltpu.VMEM((2 * NB, 2 * NB), BF16),
+            pltpu.VMEM((8, T1, F1, NB), BF16),
+            pltpu.VMEM((8, T1, F1, NB), BF16),
+            pltpu.VMEM((12, 4, 8 * T1, 2 * NB), BF16),
+            pltpu.VMEM((12, 4, 8 * T1, 2 * NB), BF16),
+            pltpu.VMEM((ROWS, QX, NB), F32),
+            pltpu.VMEM((ROWS, QX, NB), F32),
         ]
-        + phase_scratch(136, ROWS)
+        + phase_scratch(144, 40)
         + [pltpu.VMEM((2 * NB, LIST * NB), BF16)] * 2
         + [pltpu.VMEM((8 * STEP, 2 * NB), BF16), pltpu.VMEM((2 * STEP, 2 * NB), BF16)]
         + [
             pltpu.VMEM((4, 2 * NB, 3 * NB), BF16),
-            pltpu.VMEM((2 * NB, NB), BF16),
-            pltpu.VMEM((2, 2 * NB, NB), BF16),
-            pltpu.VMEM((4, 6 * NB, NB), BF16),
+            pltpu.VMEM((4, 2, 2 * NB, 2 * NB), BF16),
             pltpu.VMEM((3, 8 * F2, 2 * NB), BF16),
             pltpu.VMEM((2, 2 * F2, 2 * NB), BF16),
-            pltpu.VMEM((8 * F2, 6 * NB), BF16),
-            pltpu.VMEM((3, 8 * F2, NB), F32),
+            pltpu.VMEM((12, 8 * F2, NB), F32),
             pltpu.VMEM((8 * F2, 9 * NB), BF16),
             pltpu.VMEM((288, 8 * 3 * NB), BF16),
             pltpu.VMEM((8, 56, 3 * NB), F32),
+            pltpu.VMEM((8, T1, F1, NB), F32),
+            pltpu.VMEM((2, T1, F1, NB), F32),
+            pltpu.VMEM((2, T2, F2, NB), F32),
+            pltpu.VMEM((9 * NB, 3 * NB), BF16),
+            pltpu.VMEM((8, T1, F1, NB), F32),
+            pltpu.VMEM((8, F1 // 2, NB), F32),
+            pltpu.VMEM((8, F1 // 2, NB), F32),
+            pltpu.SemaphoreType.DMA((4,)),
+            pltpu.SemaphoreType.DMA((2,)),
         ],
         compiler_params=pltpu.CompilerParams(collective_id=0, has_side_effects=True, **params),
         name="main",
     )(
-        jnp.asarray(theta_weights()),
         index,
         child_out,
         table_child,
         table_parent,
+        jnp.asarray(theta_down()),
         jnp.asarray(phi_up()),
-        jnp.asarray(theta_down()),
+        *[jnp.asarray(theta_up(*block[:4])) for block in BLOCKS],
         jnp.asarray(phi_down()),
     )
 
     return pl.pallas_call(
         final_kernel,
+        grid=(T1 // FINAL,),
         out_shape=shape(8, T1, F1, NB),
-        in_specs=[VM] * 3,
-        out_specs=VM,
+        in_specs=[
+            pl.BlockSpec((1, NB), lambda n: (0, 0)),
+            pl.BlockSpec((8, F1, 2 * NB), lambda n: (0, 0, 0)),
+            pl.BlockSpec((8, FINAL, F1, NB), lambda n: (0, n, 0, 0)),
+        ],
+        out_specs=pl.BlockSpec((8, FINAL, F1, NB), lambda n: (0, n, 0, 0)),
         scratch_shapes=[pltpu.VMEM((2, 8 * F1, 2 * NB), BF16), pltpu.VMEM((8, 2 * NB, NB), BF16)]
         + phase_scratch(64, 16),
         compiler_params=pltpu.CompilerParams(**params),

time: 67.3 us -> 56.1 us (0.83); the launches traced: 67 us -> 55 us
  Pallas kernels: 64.2 us -> 55 us
  local copies, waits for them, and re-layouts: 2.83 us -> 0 us
    pallas_call x1, Pallas kernels: 55.7 us -> 46.9 us  [per_device(): pl.pallas_call(main_kernel, out_shape=(shape(8, F1, 2 * NB), shape(8, T1,...]
    unnamed x2 -> x0, local copies, waits for them, and re-layouts: 2.83 us -> none
where the time goes in v2:
time: 56.1 us; the launch traced here: 55 us
  Pallas kernels  55 us (98%)
    pallas_call x1, Pallas kernels, per_device(): pl.pallas_call(main_kernel, out_shape=(shape(8, F1, 2 * NB), shape(8, T1,...  46.9 us
    pallas_call x1, Pallas kernels, per_device(): pl.pallas_call(final_kernel, grid=(T1 // FINAL,), out_shape=shape(8, T1,...  6.37 us
    pallas_call x1, Pallas kernels, per_device(): pl.pallas_call(index_kernel, out_shape=jax.ShapeDtypeStruct((INDEX_ROWS,...  1.74 us

profile of v2, /device:TPU:3, one launch (start us, length us, event | category | flops | bytes accessed | tf_op | source)
XLA Modules:
  0.0 55.0 jit_solution(16577767140895290876)
XLA Ops:
  0.0 1.7 %index.1.index_ref = s32[168,128]{1,0:T(8,128)} custom-call(s32[1,128]{1,0:T(1,128)} %bitcast.5, s32[12,128]{1,0:T(8,128)} %bitcast.3, s32[12,128]{1,0:T(8,128)} %bitcast.4, s32[16,12]{1,0:T(8,128)} %sp_ref.1, s32[16,12]{1,0:T(8,128)} %kp_ref.1), custom_call_target="tpu_custom_call" | custom-call | tf_op jit(solution)/shard_map/index/pallas_call | solution.py:691
  1.7 46.9 %main.1 = (f32[8,48,256]{2,1,0:T(8,128)}, f32[8,12,48,128]{3,2,1,0:T(8,128)}) custom-call(s32[168,128]{1,0:T(8,128)} %index.1.index_ref, f32[8,12,48,128]{3,2,1,0:T(8,128)} %x_far.1, f32[2,12,48,128]{3,2,1,0:T(8,128)} %tc_far.1, f32[2,22,88,128]{3,2,1,0:T(8,128)} %tp_far.1, bf16[1152,384]{1,0:T(8,128)(2,1)} %constant.14.clone.theta_far, ...), custom_call_target="tpu_custom_call" | custom-call | tf_op jit(solution)/shard_map/main/pallas_call | solution.py:700
  48.6 6.4 %final.1 = f32[8,12,48,128]{3,2,1,0:T(8,128)} custom-call(s32[1,128]{1,0:T(1,128)} %bitcast.6, f32[8,48,256]{2,1,0:T(8,128)} %get-tuple-element.7.w_ref, f32[8,12,48,128]{3,2,1,0:T(8,128)} %get-tuple-element.8.local_ref), custom_call_target="tpu_custom_call" | custom-call | tf_op jit(solution)/shard_map/final/pallas_call | solution.py:754

commit v3 on v2

--- a/solution.py
+++ b/solution.py
@@ -154,19 +154,38 @@
     return jnp.where(north == 1, quarter, -quarter)
 
 
-def fill_phases(slot, tables, rows, first_plus, first_minus, polar_first, polar_rows, period):
-    plus_c, plus_s, minus_c, minus_s, polar_c, polar_s = tables
-    octant = jnp.broadcast_to(slot // 16, (rows, NB))
-    shift = octant_shift(octant, period // 8)
-    row = iota((rows, NB), 0)
-    plus_c[...], plus_s[...] = ring_phase(row + first_plus, shift, period)
-    minus_c[...], minus_s[...] = ring_phase(-(row + first_minus), -shift, period)
-    upper = jnp.broadcast_to(slot // 64, (polar_rows, NB))
-    sign = jnp.where(upper == 1, WAVE, -WAVE)
-    polar = (iota((polar_rows, NB), 0) + polar_first).astype(F32) + 0.5
-    phase = sign * jnp.cos(polar * (2.0 * math.pi / period))
-    polar_c[...] = jnp.cos(phase)
-    polar_s[...] = jnp.sin(phase)
+UP_ROWS, DOWN_ROWS = (144, 40), (64, 16)
+
+
+def table_rows(rows):
+    starts = [0, rows[0], 2 * rows[0], 3 * rows[0], 4 * rows[0], 4 * rows[0] + rows[1]]
+    return starts, 4 * rows[0] + 2 * rows[1]
+
+
+def views(ref, rows):
+    starts, end = table_rows(rows)
+    return [ref.at[low:high] for low, high in zip(starts, starts[1:] + [end])]
+
+
+def fill_phases(octant, o_ref, rows, first_plus, first_minus, polar_first, period):
+    starts, end = table_rows(rows)
+    lane = iota((8, NB), 1)
+    shift = octant_shift(lane // 16, period // 8)
+    sign = jnp.where(lane // 64 == 1, WAVE, -WAVE)
+    for n in range(0, max(rows), 128):
+        row = n + 8 * lax.rem(lane, 16) + iota((8, NB), 0)
+        polar = (row + polar_first).astype(F32) + 0.5
+        phase = sign * jnp.cos(polar * (2.0 * math.pi / period))
+        packed = (
+            *ring_phase(row + first_plus, shift, period),
+            *ring_phase(-(row + first_minus), -shift, period),
+            jnp.cos(phase),
+            jnp.sin(phase),
+        )
+        for k in range(6):
+            for j in range(min(16, (rows[k // 4] - n) // 8)):
+                spread = jnp.take_along_axis(packed[k], octant * 16 + j, axis=1)
+                o_ref[starts[k] + n + 8 * j : starts[k] + n + 8 * j + 8, :] = spread
 
 
 def times(ar, ai, br, bi):
@@ -176,7 +195,13 @@
 INDEX_ROWS = NB + 40
 
 
-def index_kernel(slot_ref, sc_ref, kc_ref, sp_ref, kp_ref, o_ref, wide):
+def index_kernel(slot_ref, sc_ref, kc_ref, sp_ref, kp_ref, o_ref, up_ref, down_ref, wide):
+    theta, phi = lax.axis_index("theta"), lax.axis_index("phi")
+    i0, k0 = theta * T2, phi * F2
+    fill_phases(iota((8, NB), 1) // 16, up_ref, UP_ROWS, i0 + k0 - 14, k0 - i0 - 35, i0 - 6, PH2)
+    t0, f0 = theta * T1, phi * F1
+    octant = jnp.broadcast_to(slot_ref[...] // 16, (8, NB))
+    fill_phases(octant, down_ref, DOWN_ROWS, t0 + f0, f0 - t0 - 11, t0, PH1)
     o_ref[0:NB, :] = jnp.broadcast_to(slot_ref[...], (NB, NB)).T
     o_ref[NB : NB + 8, :] = jnp.broadcast_to(slot_ref[...], (8, NB))
     lane, row = iota((16, NB), 1), iota((16, NB), 0)
@@ -211,10 +236,7 @@
     return merge(even, merge(first, pairs[0], pairs[1], 96), merge(second, pairs[2], late, 96), 112)
 
 
-def up_setup(slot_col, load_x, x_ref, up_ref, lhs, order, xh, xl, vh, vl, er_ref, ei_ref, tables):
-    theta, phi = lax.axis_index("theta"), lax.axis_index("phi")
-    i0, k0 = theta * T2, phi * F2
-    fill_phases(iota((1, NB), 1), tables, 144, i0 + k0 - 14, k0 - i0 - 35, i0 - 6, 40, PH2)
+def up_turn(slot_col, load_x, x_ref, lhs, order, xh, xl):
     block = flags(iota((NB, NB), 1) == slot_col)
     order[...] = jnp.zeros_like(order)
     order[0:NB, 0:NB] = block
@@ -232,6 +254,9 @@
         return carry
 
     lax.fori_loop(0, 8, turn, 0)
+
+
+def up_columns(count, where, up_ref, xh, xl, vh, vl, er_ref, ei_ref, tables):
     plus_c, plus_s, minus_c, minus_s, polar_c, polar_s = tables
     left = iota((8, NB), 0) >= 3
 
@@ -240,7 +265,8 @@
         edge = jnp.where(left, table[pl.ds(start, 8), :], table[pl.ds(start + 97, 8), :])
         return jnp.concatenate([main, edge], axis=0)
 
-    def two_rows(n, carry):
+    def two_rows(k, carry):
+        n = where(k)
         for c in range(4):
             outs = []
             for h in range(2):
@@ -262,7 +288,7 @@
             er_ref[r], ei_ref[r] = e
         return carry
 
-    lax.fori_loop(0, 6, two_rows, 0)
+    lax.fori_loop(0, count, two_rows, 0)
 
 
 def up_blocks(numbers, theta_refs, z_ref, vh, vl, er_ref, ei_ref):
@@ -293,7 +319,7 @@
                         z_ref[tile, c + 4 * h, rows, :] = merge_tile(pairs[h], count)
         return carry
 
-    lax.fori_loop(0, 12, group, 0)
+    lax.fori_loop(0, 12, group, 0, unroll=4)
 
 
 def neighbours():
@@ -355,8 +381,10 @@
             guarded(has, copy.start)
 
 
-def finish(around, source, landing, send_sem, recv_sem):
+def finish(around, wanted, source, landing, send_sem, recv_sem):
     for n, (dt, df, has, device) in enumerate(around):
+        if not wanted(dt):
+            continue
         copy = pltpu.make_async_remote_copy(
             src_ref=source(dt, df),
             dst_ref=landing[(dt, df)],
@@ -384,8 +412,9 @@
         cut = pl.ds(2 * g, 2)
         for c in range(8):
             hi, lo = halves(x_ref[c, cut].reshape(STEP, NB))
-            lx[c * STEP : (c + 1) * STEP, 0:NB] = hi
-            lx[c * STEP : (c + 1) * STEP, NB : 2 * NB] = lo
+            at = slice((2 * (c % 4) + c // 4) * STEP, (2 * (c % 4) + c // 4 + 1) * STEP)
+            lx[at, 0:NB] = hi
+            lx[at, NB : 2 * NB] = lo
         for c in range(2):
             hi, lo = halves(t_ref[c, cut].reshape(STEP, NB))
             lt[c * STEP : (c + 1) * STEP, 0:NB] = hi
@@ -394,18 +423,18 @@
         for pair in range(LIST // 2):
             both = slice(pair * 2 * NB, (pair + 1) * 2 * NB)
             tt = jnp.dot(lt[...], hot_k[:, both], preferred_element_type=F32)
-            xx = jnp.dot(lx[...], hot_s[:, both], preferred_element_type=F32)
-            for h in range(2):
-                one = slice(h * NB, h * NB + NB)
-                a, b = tt[:STEP, one], tt[STEP:, one]
-                for c in range(4):
-                    u = xx[c * STEP : (c + 1) * STEP, one]
-                    v = xx[(c + 4) * STEP : (c + 5) * STEP, one]
-                    re, im = times(u, v, a, b)
-                    total[c] = re if total[c] is None else total[c] + re
-                    total[c + 4] = im if total[c + 4] is None else total[c + 4] + im
-        for c in range(8):
-            o_ref[c, cut] = total[c].reshape(2, F1, NB)
+            for c in range(4):
+                xx = jnp.dot(lx[2 * c * STEP : (2 * c + 2) * STEP, :], hot_s[:, both], preferred_element_type=F32)
+                found = []
+                for h in range(2):
+                    one = slice(h * NB, h * NB + NB)
+                    found.append(times(xx[:STEP, one], xx[STEP:, one], tt[:STEP, one], tt[STEP:, one]))
+                for h in range(2):
+                    value = (found[0][h] + found[1][h]).reshape(2, F1, NB)
+                    if pair == 0:
+                        o_ref[c + 4 * h, cut] = value
+                    else:
+                        o_ref[c + 4 * h, cut] += value
         return carry
 
     lax.fori_loop(low, high, step, 0)
@@ -421,36 +450,22 @@
     return source
 
 
-def up_join(around, z_ref, landing):
+def up_join(z_ref, tile, left, right):
     sub = iota((8, NB), 0)
-
-    def from_left(tile, block):
-        z_ref[tile, :, 0:8, :] += jnp.where((sub >= 1) & (sub <= 3), pltpu.roll(block, 1, 1), 0.0)
-
-    def from_right(tile, block):
-        z_ref[tile, :, F2 - 8 : F2, :] += jnp.where(sub >= 3, block, 0.0)
-
-    for tile in range(3):
-        from_left(tile, landing[(0, -1)][tile])
-        from_right(tile, landing[(0, 1)][tile])
-
-    @pl.when(around[0][2])
-    def _():
-        z_ref[0, :, 0:F2, :] += landing[(-1, 0)][...]
-        from_left(0, landing[(-1, -1)][...])
-        from_right(0, landing[(-1, 1)][...])
-
-    @pl.when(around[-1][2])
-    def _():
-        z_ref[2, :, 0:F2, :] += landing[(1, 0)][...]
-        from_left(2, landing[(1, -1)][...])
-        from_right(2, landing[(1, 1)][...])
-
-
-PAIRS = T2 // 2
-
-
-def parent_setup(src_ref, kind_ref, hot_x, hot_t, sums):
+    z_ref[tile, :, 0:8, :] += jnp.where((sub >= 1) & (sub <= 3), pltpu.roll(left, 1, 1), 0.0)
+    z_ref[tile, :, F2 - 8 : F2, :] += jnp.where(sub >= 3, right, 0.0)
+
+
+def up_join_outer(around, z_ref, landing):
+    for side, has, tile in ((-1, around[0][2], 0), (1, around[-1][2], 2)):
+
+        @pl.when(has)
+        def _(side=side, tile=tile):
+            z_ref[tile, :, 0:F2, :] += landing[(side, 0)][...]
+            up_join(z_ref, tile, landing[(side, -1)][...], landing[(side, 1)][...])
+
+
+def parent_setup(src_ref, kind_ref, hot_x, hot_t):
     row = iota((NB, NB), 0)
     for jj in range(4):
         keep = first_of_pair(jj)
@@ -467,46 +482,58 @@
             hot_t[jj, 1, cut, 0:NB] = early
             hot_t[jj, 0, cut, NB : 2 * NB] = flags(late & keep)
             hot_t[jj, 1, cut, NB : 2 * NB] = flags(late & jnp.logical_not(keep))
-    sums[11] = jnp.zeros_like(sums[11])
-
-
-def parent_rows(z_ref, t_ref, hot_x, hot_t, lx, lt, sums):
-    for tile in range(3):
+
+
+def parent_rows(tiles, z_ref, t_ref, hot_x, hot_t, lx, lt, sums):
+    lane = iota((1, NB), 1)
+    halfway = [lax.rem(lane + 128 - 16 * q, 64) < 32 for q in range(2)]
+    keeps = [first_of_pair(jj) for jj in range(4)]
+    for tile in tiles:
         for c in range(8):
             hi, lo = halves(z_ref[tile, c, 0:F2, :])
-            lx[tile, c * F2 : (c + 1) * F2, 0:NB] = hi
-            lx[tile, c * F2 : (c + 1) * F2, NB : 2 * NB] = lo
-
-    def pair(n, carry):
-        tile, jj = n // 4, lax.rem(n, 4)
-        keep = first_of_pair(jj)
-        for r in range(2):
-            for c in range(2):
-                hi, lo = halves(t_ref[c, 2 * n + r])
-                lt[r, c * F2 : (c + 1) * F2, 0:NB] = hi
-                lt[r, c * F2 : (c + 1) * F2, NB : 2 * NB] = lo
-        t0 = jnp.dot(lt[0], hot_t[jj, 0], preferred_element_type=F32)
-        t1 = jnp.dot(lt[1], hot_t[jj, 1], preferred_element_type=F32)
-        tt = [t0[:, 0:NB], t1[:, 0:NB], t0[:, NB : 2 * NB] + t1[:, NB : 2 * NB]]
-        xx = jnp.dot(lx[tile], hot_x[jj], preferred_element_type=F32)
+            at = slice((2 * (c % 4) + c // 4) * F2, (2 * (c % 4) + c // 4 + 1) * F2)
+            lx[tile, at, 0:NB] = hi
+            lx[tile, at, NB : 2 * NB] = lo
+
+    def quad(tile, q):
+        tables = []
+        for m in range(2):
+            jj = 2 * q + m
+            for r in range(2):
+                for c in range(2):
+                    hi, lo = halves(t_ref[c, jnp.minimum(8 * tile + 2 * jj + r, T2 - 1)])
+                    lt[m, r, c * F2 : (c + 1) * F2, 0:NB] = hi
+                    lt[m, r, c * F2 : (c + 1) * F2, NB : 2 * NB] = lo
+            t0 = jnp.dot(lt[m, 0], hot_t[jj, 0], preferred_element_type=F32)
+            t1 = jnp.dot(lt[m, 1], hot_t[jj, 1], preferred_element_type=F32)
+            tables.append([t0[:, 0:NB], t1[:, 0:NB], t0[:, NB : 2 * NB] + t1[:, NB : 2 * NB]])
         for c in range(4):
-            parts = []
-            for k in range(3):
-                one = slice(k * NB, k * NB + NB)
-                u = xx[c * F2 : (c + 1) * F2, one]
-                v = xx[(c + 4) * F2 : (c + 5) * F2, one]
-                parts.append(times(u, v, tt[k][:F2], tt[k][F2:]))
+            pairs = ([], [])
+            for m in range(2):
+                jj, tt = 2 * q + m, tables[m]
+                xx = jnp.dot(lx[tile, 2 * c * F2 : (2 * c + 2) * F2, :], hot_x[jj], preferred_element_type=F32)
+                parts = []
+                for k in range(3):
+                    one = slice(k * NB, k * NB + NB)
+                    parts.append(times(xx[0:F2, one], xx[F2 : 2 * F2, one], tt[k][:F2], tt[k][F2:]))
+                for h in range(2):
+                    pairs[h].append(merge(keeps[jj], parts[0][h], parts[1][h], 64) + parts[2][h])
             for h in range(2):
-                value = merge(keep, parts[0][h], parts[1][h], 64) + parts[2][h]
-                sums[n, (c + 4 * h) * F2 : (c + 4 * h + 1) * F2, :] = value
+                at = slice((c + 4 * h) * F2, (c + 4 * h + 1) * F2)
+                sums[2 * tile + q, at, :] = merge(halfway[q], pairs[h][0], pairs[h][1], 96)
+
+    def one_tile(k, carry):
+        for q in range(2):
+            quad(tiles[0] + 2 * k, q)
         return carry
 
-    lax.fori_loop(0, PAIRS, pair, 0)
+    lax.fori_loop(0, len(tiles), one_tile, 0)
 
 
 def parent_down(sums, theta_ref, phi_ref, w_ref, ld, rd):
+    even = lax.rem(iota((1, NB), 1), 32) < 16
     for tile in range(3):
-        hi, lo = halves(merge_tile([sums[4 * tile + m] for m in range(4)], 4))
+        hi, lo = halves(merge(even, sums[2 * tile], sums[2 * tile + 1], 112))
         ld[:, (3 * tile) * NB : (3 * tile + 1) * NB] = hi
         ld[:, (3 * tile + 1) * NB : (3 * tile + 2) * NB] = lo
         ld[:, (3 * tile + 2) * NB : (3 * tile + 3) * NB] = hi
@@ -573,18 +600,18 @@
         wo_ref[:, F1 - 8 : F1, cut] += jnp.where(keep8 & (sub8 >= 5), pltpu.roll(landing[(1, 1)][...], 64, 2), 0.0)
 
 
-EARLY = 2
+EARLY = 3
 
 
 def main_kernel(
-    index_ref, x_far, tc_far, tp_far, theta_far, up_ref, ta_ref, tb_ref, tc2_ref, td_ref, phi_ref, wo_ref, local_far, *scratch
+    index_ref, table_ref, x_far, tc_far, tp_far, theta_far, up_ref, ta_ref, tb_ref, tc2_ref, td_ref, phi_ref, wo_ref, local_far, *scratch
 ):
     up_land, down_land, up_sems, down_sems = scratch[0:8], scratch[8:16], scratch[16:18], scratch[18:20]
     z_ref, lhs, order, xh, xl, vh, vl, er_ref, ei_ref = scratch[20:29]
-    tables = scratch[29:35]
-    hot_s, hot_k, lx, lt = scratch[35:39]
-    hot_x, hot_t, plx, plt, sums, ld, rd, w_ref = scratch[39:47]
-    x_ref, tc_ref, tp_ref, theta_ref, local_ref, send_up, send_down, load_sem, store_sem = scratch[47:56]
+    tables = views(table_ref, UP_ROWS)
+    hot_s, hot_k, lx, lt = scratch[29:33]
+    hot_x, hot_t, plx, plt, sums, ld, rd, w_ref = scratch[33:41]
+    x_ref, tc_ref, tp_ref, theta_ref, local_ref, send_up, send_down, load_sem, store_sem = scratch[41:50]
     loads = [
         pltpu.make_async_copy(far, near, load_sem.at[n])
         for n, (far, near) in enumerate(
@@ -601,33 +628,41 @@
     up_landing, down_landing = dict(zip(keys, up_land)), dict(zip(keys, down_land))
     around = neighbours()
     greet(around)
-    up_setup(index_ref[0:NB, :], loads[0], x_ref, up_ref, lhs, order, xh, xl, vh, vl, er_ref, ei_ref, tables)
+    up_turn(index_ref[0:NB, :], loads[0], x_ref, lhs, order, xh, xl)
+    column_refs = (up_ref, xh, xl, vh, vl, er_ref, ei_ref, tables)
+    up_columns(4, lambda k: k + 2 * (k // 2), *column_refs)
     shared = ((ta_ref, tb_ref, tc2_ref, td_ref), z_ref, vh, vl, er_ref, ei_ref)
     up_blocks((0, 1), *shared)
-    child_setup(index_ref.at[NB + 8 : NB + 24], index_ref.at[NB + 24 : NB + 40], hot_s, hot_k)
     met(around)
     source = up_source(z_ref)
     exchange(around, lambda dt: dt != 0, source, up_landing, *up_sems)
+    up_columns(2, lambda k: k + 2, *column_refs)
     up_blocks((2, 3), *shared)
+    exchange(around, lambda dt: dt == 0, source, up_landing, *up_sems)
+    child_setup(index_ref.at[NB + 8 : NB + 24], index_ref.at[NB + 24 : NB + 40], hot_s, hot_k)
+    children = (x_ref, tc_ref, local_ref, hot_s, hot_k, lx, lt)
     rd[...] = jnp.zeros_like(rd)
-    parent_setup(index_ref.at[NB + 20 : NB + 22], index_ref.at[NB + 36 : NB + 38], hot_x, hot_t, sums)
-    exchange(around, lambda dt: dt == 0, source, up_landing, *up_sems)
-    children = (x_ref, tc_ref, local_ref, hot_s, hot_k, lx, lt)
+    parent_setup(index_ref.at[NB + 20 : NB + 22], index_ref.at[NB + 36 : NB + 38], hot_x, hot_t)
     loads[1].wait()
     child_steps(0, EARLY, *children)
     stores[0].start()
-    finish(around, source, up_landing, *up_sems)
-    up_join(around, z_ref, up_landing)
+    finish(around, lambda dt: dt == 0, source, up_landing, *up_sems)
+    for tile in range(3):
+        up_join(z_ref, tile, up_landing[(0, -1)][tile], up_landing[(0, 1)][tile])
     loads[2].wait()
+    parent = (z_ref, tp_ref, hot_x, hot_t, plx, plt, sums)
+    parent_rows((1,), *parent)
+    finish(around, lambda dt: dt != 0, source, up_landing, *up_sems)
+    up_join_outer(around, z_ref, up_landing)
+    parent_rows((0, 2), *parent)
     loads[3].wait()
-    parent_rows(z_ref, tp_ref, hot_x, hot_t, plx, plt, sums)
     parent_down(sums, theta_ref, phi_ref, w_ref, ld, rd)
     down_pack(w_ref, send_up, send_down)
     source = down_source(w_ref, send_up, send_down)
     exchange(around, lambda dt: True, source, down_landing, *down_sems)
     child_steps(EARLY, T1 // 2, *children)
     stores[1].start()
-    finish(around, source, down_landing, *down_sems)
+    finish(around, lambda dt: True, source, down_landing, *down_sems)
     down_join(around, w_ref, wo_ref, down_landing)
     for store in stores:
         store.wait()
@@ -636,14 +671,11 @@
 FINAL = 2
 
 
-def final_kernel(slot_ref, w_ref, local_ref, o_ref, lw, spread, *tables):
-    plus_c, plus_s, minus_c, minus_s, polar_c, polar_s = tables
+def final_kernel(slot_ref, table_ref, w_ref, local_ref, o_ref, lw, spread):
+    plus_c, plus_s, minus_c, minus_s, polar_c, polar_s = views(table_ref, DOWN_ROWS)
 
     @pl.when(pl.program_id(0) == 0)
     def _():
-        theta, phi = lax.axis_index("theta"), lax.axis_index("phi")
-        t0, f0 = theta * T1, phi * F1
-        fill_phases(slot_ref[...], tables, 64, t0 + f0, f0 - t0 - 11, t0, 16, PH1)
         row = iota((NB, NB), 0)
         parent = lax.rem(jnp.broadcast_to(slot_ref[...], (NB, NB)), 16)
         for j in range(8):
@@ -673,10 +705,6 @@
             o_ref[c + 4, n] = im + local_ref[c + 4, n]
 
 
-def phase_scratch(rows, polar_rows):
-    return [pltpu.VMEM((rows, NB), F32)] * 4 + [pltpu.VMEM((polar_rows, NB), F32)] * 2
-
-
 def shape(*dims):
     return jax.ShapeDtypeStruct(dims, F32)
 
@@ -688,11 +716,15 @@
 def per_device(child_out, child_slot, sources_child, kinds_child, table_child, sources_parent, kinds_parent, table_parent):
     slot_row = child_slot.reshape(1, NB)
     params = dict(vmem_limit_bytes=60 * 1024 * 1024)
-    index = pl.pallas_call(
+    index, up_table, down_table = pl.pallas_call(
         index_kernel,
-        out_shape=jax.ShapeDtypeStruct((INDEX_ROWS, NB), jnp.int32),
+        out_shape=(
+            jax.ShapeDtypeStruct((INDEX_ROWS, NB), jnp.int32),
+            shape(table_rows(UP_ROWS)[1], NB),
+            shape(table_rows(DOWN_ROWS)[1], NB),
+        ),
         in_specs=[VM] * 5,
-        out_specs=VM,
+        out_specs=(VM, VM, VM),
         scratch_shapes=[pltpu.VMEM((NB, NB), jnp.int32)],
         name="index",
     )(slot_row, sources_child.T, kinds_child.T, sources_parent, kinds_parent)
@@ -700,7 +732,7 @@
     wo, local = pl.pallas_call(
         main_kernel,
         out_shape=(shape(8, F1, 2 * NB), shape(8, T1, F1, NB)),
-        in_specs=[VM] + [ANY] * 4 + [VM] * 6,
+        in_specs=[VM] * 2 + [ANY] * 4 + [VM] * 6,
         out_specs=(VM, ANY),
         scratch_shapes=landing_scratch((8, F2, NB), (3, 8, 8, NB), (8, 8, NB))
         + landing_scratch((8, F1 // 2, NB), (8, 8, 2 * NB), (8, 8, NB))
@@ -716,15 +748,14 @@
             pltpu.VMEM((ROWS, QX, NB), F32),
             pltpu.VMEM((ROWS, QX, NB), F32),
         ]
-        + phase_scratch(144, 40)
         + [pltpu.VMEM((2 * NB, LIST * NB), BF16)] * 2
         + [pltpu.VMEM((8 * STEP, 2 * NB), BF16), pltpu.VMEM((2 * STEP, 2 * NB), BF16)]
         + [
             pltpu.VMEM((4, 2 * NB, 3 * NB), BF16),
             pltpu.VMEM((4, 2, 2 * NB, 2 * NB), BF16),
             pltpu.VMEM((3, 8 * F2, 2 * NB), BF16),
-            pltpu.VMEM((2, 2 * F2, 2 * NB), BF16),
-            pltpu.VMEM((12, 8 * F2, NB), F32),
+            pltpu.VMEM((2, 2, 2 * F2, 2 * NB), BF16),
+            pltpu.VMEM((6, 8 * F2, NB), F32),
             pltpu.VMEM((8 * F2, 9 * NB), BF16),
             pltpu.VMEM((288, 8 * 3 * NB), BF16),
             pltpu.VMEM((8, 56, 3 * NB), F32),
@@ -742,6 +773,7 @@
         name="main",
     )(
         index,
+        up_table,
         child_out,
         table_child,
         table_parent,
@@ -757,15 +789,15 @@
         out_shape=shape(8, T1, F1, NB),
         in_specs=[
             pl.BlockSpec((1, NB), lambda n: (0, 0)),
+            pl.BlockSpec((table_rows(DOWN_ROWS)[1], NB), lambda n: (0, 0)),
             pl.BlockSpec((8, F1, 2 * NB), lambda n: (0, 0, 0)),
             pl.BlockSpec((8, FINAL, F1, NB), lambda n: (0, n, 0, 0)),
         ],
         out_specs=pl.BlockSpec((8, FINAL, F1, NB), lambda n: (0, n, 0, 0)),
-        scratch_shapes=[pltpu.VMEM((2, 8 * F1, 2 * NB), BF16), pltpu.VMEM((8, 2 * NB, NB), BF16)]
-        + phase_scratch(64, 16),
+        scratch_shapes=[pltpu.VMEM((2, 8 * F1, 2 * NB), BF16), pltpu.VMEM((8, 2 * NB, NB), BF16)],
         compiler_params=pltpu.CompilerParams(**params),
         name="final",
-    )(slot_row, wo, local)
+    )(slot_row, down_table, wo, local)
 
 
 def solution(mesh):

time: 56.1 us -> 49.6 us (0.88); the launches traced: 55 us -> 49.3 us
  Pallas kernels: 55 us -> 49.3 us
    pallas_call x1, Pallas kernels: 46.9 us -> 41.4 us  [per_device(): pl.pallas_call(main_kernel, out_shape=(shape(8, F1, 2 * NB), shape(8, T1,...]
where the time goes in v3:
time: 49.6 us; the launch traced here: 49.3 us
  Pallas kernels  49.3 us (99%)
    pallas_call x1, Pallas kernels, per_device(): pl.pallas_call(main_kernel, out_shape=(shape(8, F1, 2 * NB), shape(8, T1,...  41.4 us
    pallas_call x1, Pallas kernels, per_device(): pl.pallas_call(final_kernel, grid=(T1 // FINAL,), out_shape=shape(8, T1,...  5.86 us
    pallas_call x1, Pallas kernels, per_device(): pl.pallas_call(index_kernel, out_shape=(jax.ShapeDtypeStruct((INDEX_ROWS,...  2.05 us

profile of v3, /device:TPU:3, one launch (start us, length us, event | category | flops | bytes accessed | tf_op | source)
XLA Modules:
  0.0 49.3 jit_solution(10495698355152401559)
XLA Ops:
  0.0 2.0 %index.1 = (s32[168,128]{1,0:T(8,128)}, f32[656,128]{1,0:T(8,128)}, f32[288,128]{1,0:T(8,128)}) custom-call(s32[1,128]{1,0:T(1,128)} %bitcast.5, s32[12,128]{1,0:T(8,128)} %bitcast.3, s32[12,128]{1,0:T(8,128)} %bitcast.4, s32[16,12]{1,0:T(8,128)} %sp_ref.1, s32[16,12]{1,0:T(8,128)} %kp_ref.1), custom_call_target="tpu_custom_call" | custom-call | tf_op jit(solution)/shard_map/index/pallas_call | solution.py:719
  2.0 41.4 %main.1 = (f32[8,48,256]{2,1,0:T(8,128)}, f32[8,12,48,128]{3,2,1,0:T(8,128)}) custom-call(s32[168,128]{1,0:T(8,128)} %get-tuple-element.11.index_ref, f32[656,128]{1,0:T(8,128)} %get-tuple-element.12.table_ref, f32[8,12,48,128]{3,2,1,0:T(8,128)} %x_far.1, f32[2,12,48,128]{3,2,1,0:T(8,128)} %tc_far.1, f32[2,22,88,128]{3,2,1,0:T(8,128)} %tp_far.1, ...), custom_call_target="tpu_custom_call" | custom-call | tf_op jit(solution)/shard_map/main/pallas_call | solution.py:732
  43.4 5.9 %final.1 = f32[8,12,48,128]{3,2,1,0:T(8,128)} custom-call(s32[1,128]{1,0:T(1,128)} %bitcast.6, f32[288,128]{1,0:T(8,128)} %get-tuple-element.10.table_ref, f32[8,48,256]{2,1,0:T(8,128)} %get-tuple-element.13.w_ref, f32[8,12,48,128]{3,2,1,0:T(8,128)} %get-tuple-element.14.local_ref), custom_call_target="tpu_custom_call" | custom-call | tf_op jit(solution)/shard_map/final/pallas_call | solution.py:786

commit v4 on v3

--- a/solution.py
+++ b/solution.py
@@ -440,20 +440,27 @@
     lax.fori_loop(low, high, step, 0)
 
 
-def up_source(z_ref):
+def pack_right(low, high):
+    return jnp.where(iota(low.shape, 1) < 3, low, pltpu.roll(high, 3, 1))
+
+
+def up_source(z_ref, right_outer, right_inner):
     def source(dt, df):
         if dt == 0:
-            return z_ref.at[0:3, :, F2:QX, :]
+            return right_inner if df > 0 else z_ref.at[0:3, :, F2:QX, :]
         tile = 3 if dt < 0 else 4
-        return z_ref.at[tile, :, 0:F2, :] if df == 0 else z_ref.at[tile, :, F2:QX, :]
+        if df == 0:
+            return z_ref.at[tile, :, 0:F2, :]
+        return right_outer.at[tile - 3] if df > 0 else z_ref.at[tile, :, F2:QX, :]
 
     return source
 
 
 def up_join(z_ref, tile, left, right):
-    sub = iota((8, NB), 0)
-    z_ref[tile, :, 0:8, :] += jnp.where((sub >= 1) & (sub <= 3), pltpu.roll(left, 1, 1), 0.0)
-    z_ref[tile, :, F2 - 8 : F2, :] += jnp.where(sub >= 3, right, 0.0)
+    keep = (iota((4, 8, NB), 1) >= 1) & (iota((4, 8, NB), 1) <= 3)
+    z_ref[tile, 0:4, 0:8, :] += jnp.where(keep, pltpu.roll(left, 1, 1), 0.0)
+    z_ref[tile, 4:8, 0:8, :] += jnp.where(keep, pltpu.roll(left, 6, 1), 0.0)
+    z_ref[tile, :, F2 - 8 : F2, :] += jnp.where(iota((8, NB), 0) >= 3, right, 0.0)
 
 
 def up_join_outer(around, z_ref, landing):
@@ -549,7 +556,10 @@
         w_ref[c] = jnp.dot(phi_ref[...], rd[:, cut], preferred_element_type=F32)
 
 
-def down_pack(w_ref, send_up, send_down):
+def down_pack(w_ref, send_up, send_down, send_right, send_left):
+    near, far = w_ref[0:4, F1:56, :], w_ref[4:8, F1:56, :]
+    send_right[...] = pack_right(near, far)
+    send_left[...] = jnp.where(iota(near.shape, 1) >= 5, near, pltpu.roll(far, 5, 1))
     low = iota((F1 // 2, NB), 1) < 64
     for c in range(8):
         near = w_ref[c, 0 : F1 // 2, 2 * NB : 3 * NB]
@@ -558,25 +568,31 @@
         send_down[c] = jnp.where(low, far, near)
 
 
-def down_source(w_ref, send_up, send_down):
+def down_source(send_up, send_down, send_right, send_left):
     def source(dt, df):
         if df == 0:
             return send_up if dt > 0 else send_down
-        if dt == 0:
-            return w_ref.at[:, F1:56, 0 : 2 * NB]
-        return w_ref.at[:, F1:56, 2 * NB : 3 * NB]
+        edge = send_right if df > 0 else send_left
+        return edge.at[:, :, 0 : 2 * NB] if dt == 0 else edge.at[:, :, 2 * NB : 3 * NB]
 
     return source
+
+
+def down_edges(wo_ref, cut, inside, left, right):
+    sub = iota(left.shape, 1)
+    first, last = slice(0, 8), slice(F1 - 8, F1)
+    wo_ref[0:4, first, cut] += jnp.where(inside & (sub < 3), left, 0.0)
+    wo_ref[4:8, first, cut] += jnp.where(inside & (sub < 3), pltpu.roll(left, 5, 1), 0.0)
+    wo_ref[0:4, last, cut] += jnp.where(inside & (sub >= 5), right, 0.0)
+    wo_ref[4:8, last, cut] += jnp.where(inside & (sub >= 5), pltpu.roll(right, 3, 1), 0.0)
 
 
 def down_join(around, w_ref, wo_ref, landing):
     wo_ref[...] = w_ref[:, 0:F1, 0 : 2 * NB]
-    sub = iota((8, 2 * NB), 0)
-    wo_ref[:, 0:8, :] += jnp.where(sub < 3, landing[(0, -1)][...], 0.0)
-    wo_ref[:, F1 - 8 : F1, :] += jnp.where(sub >= 5, landing[(0, 1)][...], 0.0)
+    all_lanes = iota((4, 8, 2 * NB), 2) >= 0
+    down_edges(wo_ref, slice(0, 2 * NB), all_lanes, landing[(0, -1)][...], landing[(0, 1)][...])
     half = F1 // 2
-    lane = iota((half, NB), 1)
-    sub8, lane8 = iota((8, NB), 0), iota((8, NB), 1)
+    lane, lane8 = iota((half, NB), 1), iota((4, 8, NB), 2)
 
     @pl.when(around[0][2])
     def _():
@@ -585,22 +601,21 @@
             got = landing[(-1, 0)][c]
             wo_ref[c, 0:half, cut] += jnp.where(lane < 48, got, 0.0)
             wo_ref[c, half:F1, cut] += jnp.where(lane < 48, pltpu.roll(got, 64, 1), 0.0)
-        wo_ref[:, 0:8, cut] += jnp.where((lane8 < 48) & (sub8 < 3), landing[(-1, -1)][...], 0.0)
-        wo_ref[:, F1 - 8 : F1, cut] += jnp.where((lane8 < 48) & (sub8 >= 5), landing[(-1, 1)][...], 0.0)
+        down_edges(wo_ref, cut, lane8 < 48, landing[(-1, -1)][...], landing[(-1, 1)][...])
 
     @pl.when(around[-1][2])
     def _():
         cut = slice(NB, 2 * NB)
-        keep, keep8 = (lane >= 16) & (lane < 64), (lane8 >= 16) & (lane8 < 64)
+        keep = (lane >= 16) & (lane < 64)
         for c in range(8):
             got = landing[(1, 0)][c]
             wo_ref[c, 0:half, cut] += jnp.where(keep, pltpu.roll(got, 64, 1), 0.0)
             wo_ref[c, half:F1, cut] += jnp.where(keep, got, 0.0)
-        wo_ref[:, 0:8, cut] += jnp.where(keep8 & (sub8 < 3), pltpu.roll(landing[(1, -1)][...], 64, 2), 0.0)
-        wo_ref[:, F1 - 8 : F1, cut] += jnp.where(keep8 & (sub8 >= 5), pltpu.roll(landing[(1, 1)][...], 64, 2), 0.0)
-
-
-EARLY = 3
+        left, right = pltpu.roll(landing[(1, -1)][...], 64, 2), pltpu.roll(landing[(1, 1)][...], 64, 2)
+        down_edges(wo_ref, cut, (lane8 >= 16) & (lane8 < 64), left, right)
+
+
+EARLY = 4
 
 
 def main_kernel(
@@ -612,6 +627,7 @@
     hot_s, hot_k, lx, lt = scratch[29:33]
     hot_x, hot_t, plx, plt, sums, ld, rd, w_ref = scratch[33:41]
     x_ref, tc_ref, tp_ref, theta_ref, local_ref, send_up, send_down, load_sem, store_sem = scratch[41:50]
+    right_outer, right_inner, send_right, send_left = scratch[50:54]
     loads = [
         pltpu.make_async_copy(far, near, load_sem.at[n])
         for n, (far, near) in enumerate(
@@ -634,10 +650,14 @@
     shared = ((ta_ref, tb_ref, tc2_ref, td_ref), z_ref, vh, vl, er_ref, ei_ref)
     up_blocks((0, 1), *shared)
     met(around)
-    source = up_source(z_ref)
+    for n in range(2):
+        right_outer[n] = pack_right(z_ref[3 + n, 0:4, F2:QX, :], z_ref[3 + n, 4:8, F2:QX, :])
+    source = up_source(z_ref, right_outer, right_inner)
     exchange(around, lambda dt: dt != 0, source, up_landing, *up_sems)
     up_columns(2, lambda k: k + 2, *column_refs)
     up_blocks((2, 3), *shared)
+    for n in range(3):
+        right_inner[n] = pack_right(z_ref[n, 0:4, F2:QX, :], z_ref[n, 4:8, F2:QX, :])
     exchange(around, lambda dt: dt == 0, source, up_landing, *up_sems)
     child_setup(index_ref.at[NB + 8 : NB + 24], index_ref.at[NB + 24 : NB + 40], hot_s, hot_k)
     children = (x_ref, tc_ref, local_ref, hot_s, hot_k, lx, lt)
@@ -657,8 +677,8 @@
     parent_rows((0, 2), *parent)
     loads[3].wait()
     parent_down(sums, theta_ref, phi_ref, w_ref, ld, rd)
-    down_pack(w_ref, send_up, send_down)
-    source = down_source(w_ref, send_up, send_down)
+    down_pack(w_ref, send_up, send_down, send_right, send_left)
+    source = down_source(send_up, send_down, send_right, send_left)
     exchange(around, lambda dt: True, source, down_landing, *down_sems)
     child_steps(EARLY, T1 // 2, *children)
     stores[1].start()
@@ -671,26 +691,34 @@
 FINAL = 2
 
 
-def final_kernel(slot_ref, table_ref, w_ref, local_ref, o_ref, lw, spread):
+def final_kernel(slot_ref, table_ref, w_ref, local_far, o_far, lw, spread, local_ref, o_ref, load_sem, store_sem):
+    parts = [slice(n * FINAL, n * FINAL + FINAL) for n in range(T1 // FINAL)]
+    loads = [
+        pltpu.make_async_copy(local_far.at[:, rows], local_ref.at[:, rows], load_sem.at[n])
+        for n, rows in enumerate(parts)
+    ]
+    stores = [
+        pltpu.make_async_copy(o_ref.at[:, rows], o_far.at[:, rows], store_sem.at[n])
+        for n, rows in enumerate(parts)
+    ]
+    for load in loads:
+        load.start()
     plus_c, plus_s, minus_c, minus_s, polar_c, polar_s = views(table_ref, DOWN_ROWS)
 
-    @pl.when(pl.program_id(0) == 0)
-    def _():
-        row = iota((NB, NB), 0)
-        parent = lax.rem(jnp.broadcast_to(slot_ref[...], (NB, NB)), 16)
-        for j in range(8):
-            block = flags(row == parent + 16 * j)
-            spread[j, 0:NB, :] = block
-            spread[j, NB : 2 * NB, :] = block
-        for tile in range(2):
-            for c in range(8):
-                hi, lo = halves(w_ref[c, :, tile * NB : (tile + 1) * NB])
-                lw[tile, c * F1 : (c + 1) * F1, 0:NB] = hi
-                lw[tile, c * F1 : (c + 1) * F1, NB : 2 * NB] = lo
-
-    for n in range(FINAL):
-        t = pl.program_id(0) * FINAL + n
-        wide = jnp.dot(lw[t // 8], spread[lax.rem(t, 8)], preferred_element_type=F32)
+    row = iota((NB, NB), 0)
+    parent = lax.rem(jnp.broadcast_to(slot_ref[...], (NB, NB)), 16)
+    for j in range(8):
+        block = flags(row == parent + 16 * j)
+        spread[j, 0:NB, :] = block
+        spread[j, NB : 2 * NB, :] = block
+    for tile in range(2):
+        for c in range(8):
+            hi, lo = halves(w_ref[c, :, tile * NB : (tile + 1) * NB])
+            lw[tile, c * F1 : (c + 1) * F1, 0:NB] = hi
+            lw[tile, c * F1 : (c + 1) * F1, NB : 2 * NB] = lo
+
+    def one_row(t):
+        wide = jnp.dot(lw[t // 8], spread[t % 8], preferred_element_type=F32)
         er, ei = times(
             plus_c[pl.ds(t, F1), :],
             plus_s[pl.ds(t, F1), :],
@@ -701,16 +729,24 @@
         for c in range(4):
             u, v = wide[c * F1 : (c + 1) * F1], wide[(c + 4) * F1 : (c + 5) * F1]
             re, im = times(u, v, er, -ei)
-            o_ref[c, n] = re + local_ref[c, n]
-            o_ref[c + 4, n] = im + local_ref[c + 4, n]
+            o_ref[c, t] = re + local_ref[c, t]
+            o_ref[c + 4, t] = im + local_ref[c + 4, t]
+
+    for n in range(T1 // FINAL):
+        loads[n].wait()
+        for t in range(n * FINAL, n * FINAL + FINAL):
+            one_row(t)
+        stores[n].start()
+    for store in stores:
+        store.wait()
 
 
 def shape(*dims):
     return jax.ShapeDtypeStruct(dims, F32)
 
 
-def landing_scratch(column, row, corner):
-    return [pltpu.VMEM(column, F32)] * 2 + [pltpu.VMEM(row, F32)] * 2 + [pltpu.VMEM(corner, F32)] * 4
+def landing_scratch(outer, left, right, corner_left, corner_right):
+    return [pltpu.VMEM(dims, F32) for dims in [outer] * 2 + [left, right] + [corner_left, corner_right] * 2]
 
 
 def per_device(child_out, child_slot, sources_child, kinds_child, table_child, sources_parent, kinds_parent, table_parent):
@@ -734,8 +770,8 @@
         out_shape=(shape(8, F1, 2 * NB), shape(8, T1, F1, NB)),
         in_specs=[VM] * 2 + [ANY] * 4 + [VM] * 6,
         out_specs=(VM, ANY),
-        scratch_shapes=landing_scratch((8, F2, NB), (3, 8, 8, NB), (8, 8, NB))
-        + landing_scratch((8, F1 // 2, NB), (8, 8, 2 * NB), (8, 8, NB))
+        scratch_shapes=landing_scratch((8, F2, NB), (3, 4, 8, NB), (3, 8, 8, NB), (4, 8, NB), (8, 8, NB))
+        + landing_scratch((8, F1 // 2, NB), (4, 8, 2 * NB), (4, 8, 2 * NB), (4, 8, NB), (4, 8, NB))
         + [pltpu.SemaphoreType.DMA((8,))] * 4
         + [
             pltpu.VMEM((5, 8, QX, NB), F32),
@@ -768,6 +804,10 @@
             pltpu.VMEM((8, F1 // 2, NB), F32),
             pltpu.SemaphoreType.DMA((4,)),
             pltpu.SemaphoreType.DMA((2,)),
+            pltpu.VMEM((2, 4, 8, NB), F32),
+            pltpu.VMEM((3, 4, 8, NB), F32),
+            pltpu.VMEM((4, 8, 3 * NB), F32),
+            pltpu.VMEM((4, 8, 3 * NB), F32),
         ],
         compiler_params=pltpu.CompilerParams(collective_id=0, has_side_effects=True, **params),
         name="main",
@@ -785,16 +825,17 @@
 
     return pl.pallas_call(
         final_kernel,
-        grid=(T1 // FINAL,),
         out_shape=shape(8, T1, F1, NB),
-        in_specs=[
-            pl.BlockSpec((1, NB), lambda n: (0, 0)),
-            pl.BlockSpec((table_rows(DOWN_ROWS)[1], NB), lambda n: (0, 0)),
-            pl.BlockSpec((8, F1, 2 * NB), lambda n: (0, 0, 0)),
-            pl.BlockSpec((8, FINAL, F1, NB), lambda n: (0, n, 0, 0)),
+        in_specs=[VM, VM, VM, ANY],
+        out_specs=ANY,
+        scratch_shapes=[
+            pltpu.VMEM((2, 8 * F1, 2 * NB), BF16),
+            pltpu.VMEM((8, 2 * NB, NB), BF16),
+            pltpu.VMEM((8, T1, F1, NB), F32),
+            pltpu.VMEM((8, T1, F1, NB), F32),
+            pltpu.SemaphoreType.DMA((T1 // FINAL,)),
+            pltpu.SemaphoreType.DMA((T1 // FINAL,)),
         ],
-        out_specs=pl.BlockSpec((8, FINAL, F1, NB), lambda n: (0, n, 0, 0)),
-        scratch_shapes=[pltpu.VMEM((2, 8 * F1, 2 * NB), BF16), pltpu.VMEM((8, 2 * NB, NB), BF16)],
         compiler_params=pltpu.CompilerParams(**params),
         name="final",
     )(slot_row, down_table, wo, local)

time: 49.6 us -> 46.9 us (0.946)
  Pallas kernels: 49.3 us -> 46.5 us
    pallas_call x1, Pallas kernels: 41.4 us -> 39.9 us  [per_device(): pl.pallas_call(main_kernel, out_shape=(shape(8, F1, 2 * NB), shape(8, T1,...]
    pallas_call x1, Pallas kernels: 5.86 us -> 4.55 us  [per_device(): pl.pallas_call(final_kernel, out_shape=shape(8, T1, F1, NB), in_specs=[VM...]
where the time goes in v4:
time: 46.9 us; the launch traced here: 46.5 us
  Pallas kernels  46.5 us (99%)
    pallas_call x1, Pallas kernels, per_device(): pl.pallas_call(main_kernel, out_shape=(shape(8, F1, 2 * NB), shape(8, T1,...  39.9 us
    pallas_call x1, Pallas kernels, per_device(): pl.pallas_call(final_kernel, out_shape=shape(8, T1, F1, NB), in_specs=[VM...  4.55 us
    pallas_call x1, Pallas kernels, per_device(): pl.pallas_call(index_kernel, out_shape=(jax.ShapeDtypeStruct((INDEX_ROWS,...  2.05 us

profile of v4, /device:TPU:3, one launch (start us, length us, event | category | flops | bytes accessed | tf_op | source)
XLA Modules:
  0.0 46.5 jit_solution(1204875778267539202)
XLA Ops:
  0.0 2.0 %index.1 = (s32[168,128]{1,0:T(8,128)}, f32[656,128]{1,0:T(8,128)}, f32[288,128]{1,0:T(8,128)}) custom-call(s32[1,128]{1,0:T(1,128)} %bitcast.5, s32[12,128]{1,0:T(8,128)} %bitcast.3, s32[12,128]{1,0:T(8,128)} %bitcast.4, s32[16,12]{1,0:T(8,128)} %sp_ref.1, s32[16,12]{1,0:T(8,128)} %kp_ref.1), custom_call_target="tpu_custom_call" | custom-call | tf_op jit(solution)/shard_map/index/pallas_call | solution.py:755
  2.0 39.9 %main.1 = (f32[8,48,256]{2,1,0:T(8,128)}, f32[8,12,48,128]{3,2,1,0:T(8,128)}) custom-call(s32[168,128]{1,0:T(8,128)} %get-tuple-element.11.index_ref, f32[656,128]{1,0:T(8,128)} %get-tuple-element.12.table_ref, f32[8,12,48,128]{3,2,1,0:T(8,128)} %x_far.1, f32[2,12,48,128]{3,2,1,0:T(8,128)} %tc_far.1, f32[2,22,88,128]{3,2,1,0:T(8,128)} %tp_far.1, ...), custom_call_target="tpu_custom_call" | custom-call | tf_op jit(solution)/shard_map/main/pallas_call | solution.py:768
  42.0 4.6 %final.1 = f32[8,12,48,128]{3,2,1,0:T(8,128)} custom-call(s32[1,128]{1,0:T(1,128)} %bitcast.6, f32[288,128]{1,0:T(8,128)} %get-tuple-element.10.table_ref, f32[8,48,256]{2,1,0:T(8,128)} %get-tuple-element.13.w_ref, f32[8,12,48,128]{3,2,1,0:T(8,128)} %get-tuple-element.14.local_far), custom_call_target="tpu_custom_call" | custom-call | tf_op jit(solution)/shard_map/final/pallas_call | solution.py:826

commit v5 on v4

--- a/solution.py
+++ b/solution.py
@@ -319,7 +319,7 @@
                         z_ref[tile, c + 4 * h, rows, :] = merge_tile(pairs[h], count)
         return carry
 
-    lax.fori_loop(0, 12, group, 0, unroll=4)
+    lax.fori_loop(0, 12, group, 0, unroll=3)
 
 
 def neighbours():

time: 46.9 us -> 47 us (level)
  no operation moved by 1% of the time
where the time goes in v5:
time: 47 us; the launch traced here: 46.8 us
  Pallas kernels  46.8 us (100%)
    pallas_call x1, Pallas kernels, per_device(): pl.pallas_call(main_kernel, out_shape=(shape(8, F1, 2 * NB), shape(8, T1,...  40.2 us
    pallas_call x1, Pallas kernels, per_device(): pl.pallas_call(final_kernel, out_shape=shape(8, T1, F1, NB), in_specs=[VM...  4.57 us
    pallas_call x1, Pallas kernels, per_device(): pl.pallas_call(index_kernel, out_shape=(jax.ShapeDtypeStruct((INDEX_ROWS,...  2.05 us

profile of v5, /device:TPU:3, one launch (start us, length us, event | category | flops | bytes accessed | tf_op | source)
XLA Modules:
  0.0 46.8 jit_solution(8726107440719274254)
XLA Ops:
  0.0 2.0 %index.1 = (s32[168,128]{1,0:T(8,128)}, f32[656,128]{1,0:T(8,128)}, f32[288,128]{1,0:T(8,128)}) custom-call(s32[1,128]{1,0:T(1,128)} %bitcast.5, s32[12,128]{1,0:T(8,128)} %bitcast.3, s32[12,128]{1,0:T(8,128)} %bitcast.4, s32[16,12]{1,0:T(8,128)} %sp_ref.1, s32[16,12]{1,0:T(8,128)} %kp_ref.1), custom_call_target="tpu_custom_call" | custom-call | tf_op jit(solution)/shard_map/index/pallas_call | solution.py:755
  2.0 40.2 %main.1 = (f32[8,48,256]{2,1,0:T(8,128)}, f32[8,12,48,128]{3,2,1,0:T(8,128)}) custom-call(s32[168,128]{1,0:T(8,128)} %get-tuple-element.11.index_ref, f32[656,128]{1,0:T(8,128)} %get-tuple-element.12.table_ref, f32[8,12,48,128]{3,2,1,0:T(8,128)} %x_far.1, f32[2,12,48,128]{3,2,1,0:T(8,128)} %tc_far.1, f32[2,22,88,128]{3,2,1,0:T(8,128)} %tp_far.1, ...), custom_call_target="tpu_custom_call" | custom-call | tf_op jit(solution)/shard_map/main/pallas_call | solution.py:768
  42.2 4.6 %final.1 = f32[8,12,48,128]{3,2,1,0:T(8,128)} custom-call(s32[1,128]{1,0:T(1,128)} %bitcast.6, f32[288,128]{1,0:T(8,128)} %get-tuple-element.10.table_ref, f32[8,48,256]{2,1,0:T(8,128)} %get-tuple-element.13.w_ref, f32[8,12,48,128]{3,2,1,0:T(8,128)} %get-tuple-element.14.local_far), custom_call_target="tpu_custom_call" | custom-call | tf_op jit(solution)/shard_map/final/pallas_call | solution.py:826
